TPU v7x, 256 devices: a whole 4x4x8 slice. The times are simulated.
256 devices in a mesh: band: 64 (over z, x, core), ens: 4 (over y).
Axes of the slice: x: 4, y: 4, z: 8, core: 2. Of those that a mesh axis runs over, the one named last changes fastest.
Arguments:
- grid_latent: bfloat16 [4, 8192, 1024], P('ens', 'band'), may hold values from -6 to 6
- hidden: bfloat16 [4, 2048, 1024], P('ens', 'band'), may hold values from -6 to 6
- d_updated: bfloat16 [4, 2048, 1024], P('ens', 'band'), may hold values from -6 to 6
- w_kv: bfloat16 [1024, 2048], replicated, may hold values from -0.1875 to 0.1875
- w_q: bfloat16 [1024, 1024], replicated, may hold values from -0.1875 to 0.1875
- src_gain: float32 [1024], replicated, may hold values from 0.1 to 1.9
- q_gain: float32 [1024], replicated, may hold values from 0.5 to 40
- src_index: int32 [2048, 12], P('band'), may hold values from 0 to 8191, as said below
- edge_mask: int32 [2048, 12], P('band'), may hold values from 0 to 1, as said below
Outputs:
- updated: bfloat16 [4, 2048, 1024], P('ens', 'band')
- d_grid: bfloat16 [4, 8192, 1024], P('ens', 'band')
- d_wkv_t: float32 [2048, 1024], P(('band', 'ens'))
Inputs may be any that keep to these rules, and one draw needn't show every extreme that they name: `src_index`: every edge slot of hidden node h names a grid row from max(0, (h // 32) * 128 - 32) to min(8192, (h // 32 + 1) * 128 + 32) - 1, and in every band both ends of that range are named by a valid edge. `edge_mask`: the first slot of every hidden node is valid.
All inputs are finite; a program needn't handle non-finite values.
Results may differ from a plain program's by a relative error of at most 0.013.
The roundings to bfloat16 on the way count: a program that leaves them out, or rounds other values in their place, can miss the bound.
Values may be sent and summed in bfloat16 or wider, within the bound.
A program may use at most 128 MiB of HBM per device.

v0:
```python
import math

import jax
import jax.numpy as jnp
from jax import lax
from jax.sharding import Mesh
from jax.sharding import PartitionSpec as P

HEADS = 16
K = 12
R = 32
BAND = ("band_0", "band_1", "band_2")
BAND_ENS = ("band_0", "band_1", "band_2", "ens")


EPSILON = 1e-05


def extended(cells, sides, width):
    for axis, dim in sides:
        count = lax.axis_size(axis)
        ends = count - 1
        head = lax.slice_in_dim(cells, 0, width, axis=dim)
        tail = lax.slice_in_dim(cells, cells.shape[dim] - width, cells.shape[dim], axis=dim)
        cells = jnp.concatenate(
            [
                lax.ppermute(tail, axis, [(i, (i + 1) % count) for i in range(ends)]),
                cells,
                lax.ppermute(head, axis, [((i + 1) % count, i) for i in range(ends)]),
            ],
            axis=dim,
        )
    return cells


def passed_along(value, axis, by):
    peers = lax.axis_size(axis)
    pairs = [(i, i + by) for i in range(peers) if 0 <= i + by < peers]
    return lax.ppermute(value, axis, pairs)


def own_rows(running, axes):
    for axis in axes:
        running = lax.psum_scatter(running, axis, scatter_dimension=0, tiled=True)
    return running


def in_blocks(value, dim, peers):
    shape = value.shape
    tiles = value.reshape(*shape[:dim], peers, shape[dim] // peers, *shape[dim + 1 :])
    return jnp.moveaxis(tiles, dim, 0)


def summed_on_arrival(value, axis, dim):
    peers = lax.axis_size(axis)
    tiles = lax.all_to_all(in_blocks(value, dim, peers), axis, 0, 0, tiled=True)
    return jnp.sum(tiles.astype(jnp.float32), axis=0)


def normalize(values):
    values = values.astype(jnp.float32)
    average = jnp.mean(values, axis=-1, keepdims=True)
    centred = values - average
    variance = jnp.mean(centred * centred, axis=-1, keepdims=True)
    inv_std = lax.rsqrt(variance + EPSILON)
    return (centred * inv_std, inv_std)


def times_transposed(left, right):
    return lax.dot_general(
        left, right, (((1,), (1,)), ((), ())), preferred_element_type=jnp.float32
    )


def rows_product(partial_rows, normed_rows):
    return lax.dot_general(
        partial_rows, normed_rows, (((0,), (0,)), ((), ())), preferred_element_type=jnp.float32
    )


def node_block(queries, hidden_rows, cotangent, kv_window, local_rows, valid_edges):
    node_count, features = queries.shape
    head_dim = features // HEADS
    score_scale = 1.0 / math.sqrt(head_dim)
    gathered = kv_window[local_rows]
    key_rows = gathered[..., :features].reshape(node_count, K, HEADS, head_dim)
    value_rows = gathered[..., features:].reshape(node_count, K, HEADS, head_dim)
    query_heads = queries.reshape(node_count, HEADS, head_dim)
    scores = (
        jnp.einsum("hnd,hknd->hkn", query_heads, key_rows, preferred_element_type=jnp.float32)
        * score_scale
    )
    valid = valid_edges[:, :, None] > 0
    shifted = jnp.where(valid, scores, -jnp.inf)
    row_max = jnp.max(shifted, axis=1, keepdims=True)
    exp_terms = jnp.exp(shifted - row_max)
    attn_probs = exp_terms / jnp.sum(exp_terms, axis=1, keepdims=True)
    probs_low = attn_probs.astype(jnp.bfloat16)
    attended = jnp.einsum(
        "hkn,hknd->hnd", probs_low, value_rows, preferred_element_type=jnp.float32
    )
    attended = attended.reshape(node_count, features)
    updated = (hidden_rows.astype(jnp.float32) + attended).astype(jnp.bfloat16)
    d_heads = cotangent.reshape(node_count, HEADS, head_dim)
    d_probs = jnp.einsum("hnd,hknd->hkn", d_heads, value_rows, preferred_element_type=jnp.float32)
    d_scores = attn_probs * (d_probs - jnp.sum(attn_probs * d_probs, axis=1, keepdims=True))
    d_keys = d_scores[..., None] * query_heads.astype(jnp.float32)[:, None] * score_scale
    d_values = probs_low.astype(jnp.float32)[..., None] * d_heads.astype(jnp.float32)[:, None]
    edge_grads = jnp.concatenate(
        [d_keys.reshape(node_count * K, features), d_values.reshape(node_count * K, features)],
        axis=1,
    )
    partial_value = (
        jnp.zeros((kv_window.shape[0], 2 * features), jnp.float32)
        .at[local_rows.reshape(-1)]
        .add(edge_grads)
    )
    return (updated, partial_value.astype(jnp.bfloat16))


def per_device(grid_latent, hidden, d_updated, w_kv, w_q, src_gain, q_gain, src_index, edge_mask):
    grid_rows = grid_latent.shape[1]
    standard, inv_std = normalize(grid_latent[0])
    normed = (standard * src_gain).astype(jnp.bfloat16)
    normed_window = extended(normed, ((BAND, 0),), R)
    kv_window = jnp.dot(normed_window, w_kv, preferred_element_type=jnp.float32).astype(
        jnp.bfloat16
    )
    hidden_hat, _ = normalize(hidden[0])
    hidden_normed = (hidden_hat * q_gain).astype(jnp.bfloat16)
    queries = jnp.dot(hidden_normed, w_q, preferred_element_type=jnp.float32).astype(jnp.bfloat16)
    offset = lax.axis_index(BAND) * grid_rows - R
    local_rows = src_index - offset
    updated, partial_value = node_block(
        queries, hidden[0], d_updated[0], kv_window, local_rows, edge_mask
    )
    factor = 1.0 / math.sqrt(lax.axis_size("ens") * grid_rows * lax.axis_size(BAND))
    d_window = times_transposed(partial_value, w_kv)
    back_low = passed_along(d_window[:R].astype(jnp.bfloat16), BAND, -1).astype(jnp.float32)
    back_high = passed_along(d_window[grid_rows + R :].astype(jnp.bfloat16), BAND, 1).astype(
        jnp.float32
    )
    d_normed = d_window[R : R + grid_rows]
    d_normed = d_normed.at[:R].add(back_high)
    d_normed = d_normed.at[grid_rows - R :].add(back_low)
    band_summed = own_rows(rows_product(partial_value, normed_window) * factor, BAND)
    d_wkv_t = summed_on_arrival(band_summed.astype(jnp.bfloat16), "ens", 0)
    d_scaled = d_normed * src_gain
    d_grid = inv_std * (
        d_scaled
        - jnp.mean(d_scaled, axis=-1, keepdims=True)
        - standard * jnp.mean(d_scaled * standard, axis=-1, keepdims=True)
    )
    return (updated[None], d_grid.astype(jnp.bfloat16)[None], d_wkv_t)


def solution(mesh):
    finer = Mesh(
        mesh.devices.reshape(8, 4, 2, mesh.shape["ens"]), ("band_0", "band_1", "band_2", "ens")
    )
    in_specs = (
        P("ens", BAND, None),
        P("ens", BAND, None),
        P("ens", BAND, None),
        P(),
        P(),
        P(),
        P(),
        P(BAND, None),
        P(BAND, None),
    )
    out_specs = (P("ens", BAND, None), P("ens", BAND, None), P(BAND_ENS, None))
    return jax.shard_map(
        per_device, mesh=finer, in_specs=in_specs, out_specs=out_specs, check_vma=False
    )
```

profile of v0, /device:TPU:1, one launch (start us, length us, event | category | flops | bytes accessed | tf_op | source)
XLA Modules:
  0.0 235.9 jit_solution(11287290729709078989)
XLA Ops:
  10.9 4.5 %collective-permute-start = (bf16[32,1024]{1,0:T(8,128)(2,1)S(1)}, bf16[32,1024]{1,0:T(8,128)(2,1)S(1)}, u32[]{:S(2)}, u32[]{:S(2)}) collective-permute-start(bf16[32,1024]{1,0:T(8,128)(2,1)S(1)} %get-tuple-element.35), channel_id=1, source_target_pairs={{0,4},{4,8},{8,12},{12,16},{16,20},{20,24},{24,28},{28,32},{32,36}... | collective-permute-start | bytes 196616 | tf_op jit(solution)/shard_map/ppermute | solution.py:27
  15.4 1.9 collective-permute-start.1
  24.7 3.2 %convolution_convert_fusion = bf16[192,2048]{1,0:T(8,128)(2,1)S(1)} fusion(bf16[1024,2048]{1,0:T(8,128)(2,1)} %param.16, bf16[32,1024]{1,0:T(8,128)(2,1)S(1)} %collective-permute-done.1, bf16[128,1024]{1,0:T(8,128)(2,1)S(1)} %fusion.17, bf16[32,1024]{1,0:T(8,128)(2,1)S(1)} %collective-permute-done), kind=kOutput, calls=%fused_computation.8 | convolution fusion | flops 806879232 | bytes 5373952 | tf_op jit(solution)/shard_map/dot_general | solution.py:126
  27.9 3.1 %gather_fusion = bf16[384,2048]{1,0:T(8,128)(2,1)} fusion(bf16[192,2048]{1,0:T(8,128)(2,1)S(1)} %convolution_convert_fusion, s32[1024]{0:T(1024)S(1)} %pad_clamp_fusion), kind=kCustom, calls=%fused_computation | custom fusion | bytes 3147264 | tf_op jit(solution)/shard_map/gather | solution.py:85
  31.0 3.6 %reshape.172 = bf16[32,12,2048]{2,1,0:T(8,128)(2,1)} reshape(bf16[384,2048]{1,0:T(8,128)(2,1)} %gather_fusion) | data formatting | bytes 3145728 | tf_op jit(solution)/shard_map/gather | solution.py:85
  34.7 2.8 %fusion.49 = (bf16[32,12,1024]{2,1,0:T(8,128)(2,1)}, bf16[32,12,1024]{2,1,0:T(8,128)(2,1)S(1)}) fusion(bf16[32,12,2048]{2,1,0:T(8,128)(2,1)} %reshape.172), kind=kLoop, calls=%fused_computation.84 | loop fusion | bytes 3145728 | tf_op jit(solution)/shard_map/slice | solution.py:87
  37.4 3.6 %reshape.198 = bf16[32,12,16,64]{3,2,1,0:T(8,128)(2,1)} reshape(bf16[32,12,1024]{2,1,0:T(8,128)(2,1)} %get-tuple-element.31) | data formatting | bytes 1572864 | tf_op jit(solution)/shard_map/reshape | solution.py:87
  41.0 3.3 %fusion.4 = f32[32,16,1,12]{3,2,1,0:T(1,128)} fusion(bf16[32,16,64,1]{2,3,1,0:T(2,128)(2,1)} %reshape.200, bf16[32,12,16,64]{3,2,1,0:T(8,128)(2,1)} %reshape.198), kind=kOutput, calls=%fused_computation.9 | convolution fusion | flops 786432 | bytes 876544 | tf_op jit(solution)/shard_map/hnd,hknd->hkn/dot_general | solution.py:105
  45.5 2.0 reshape.195
  47.4 2.6 %fusion.8 = f32[32,16,1,12]{3,2,1,0:T(1,128)S(1)} fusion(bf16[32,16,64,1]{2,3,1,0:T(2,128)(2,1)} %reshape.197, bf16[32,12,16,64]{3,2,1,0:T(8,128)(2,1)} %reshape.195), kind=kOutput, calls=%fused_computation.13 | convolution fusion | flops 786432 | bytes 876544 | tf_op jit(solution)/shard_map/hnd,hknd->hkn/dot_general | solution.py:90
  50.8 2.2 broadcast_multiply_fusion
  53.0 3.8 %mul.157 = f32[384,1024]{1,0:T(8,128)} reshape(f32[32,12,16,64]{3,2,1,0:T(8,128)} %broadcast_multiply_fusion) | data formatting | bytes 3145728 | tf_op jit(solution)/shard_map/mul | solution.py:108
  56.8 2.1 multiply_multiply_fusion
  58.9 3.7 %mul.153 = f32[384,1024]{1,0:T(8,128)} reshape(f32[32,12,16,64]{3,2,1,0:T(8,128)} %multiply_multiply_fusion) | data formatting | bytes 3145728 | tf_op jit(solution)/shard_map/mul | solution.py:107
  62.6 8.2 %scatter_custom_fusion = f32[192,2048]{1,0:T(8,128)} fusion(s32[384]{0:T(512)S(1)} %fusion.46, f32[384,1024]{1,0:T(8,128)} %mul.157, f32[]{:T(128)} %constant.105.clone.1, f32[384,1024]{1,0:T(8,128)} %mul.153, f32[]{:T(128)} %constant.91.clone.1), kind=kCustom, calls=%fused_computation.3 | custom fusion | flops 1572864 | bytes 4718600 | tf_op jit(solution)/shard_map/scatter-add | solution.py:116
  70.8 5.9 %convolution_multiply_fusion = f32[2048,1024]{1,0:T(8,128)} fusion(f32[192,2048]{1,0:T(8,128)} %scatter_custom_fusion, bf16[32,1024]{1,0:T(8,128)(2,1)S(1)} %copy-done.9, bf16[128,1024]{1,0:T(8,128)(2,1)S(1)} %fusion.17, bf16[32,1024]{1,0:T(8,128)(2,1)S(1)} %copy-done.7), kind=kOutput, calls=%fused_computation.2 | convolution fusion | flops 808976384 | bytes 10354688 | tf_op jit(solution)/shard_map/dot_general | solution.py:76
  76.8 98.8 %reduce-scatter.4.cloned.1.call-done = f32[256,1024]{1,0:T(8,128)} async-done(((f32[2048,1024]{1,0:T(8,128)}), f32[256,1024]{1,0:T(8,128)}) %reduce-scatter.4.cloned.1.call-update) | async-done | bytes 1048592 | tf_op jit(solution)/shard_map/reduce_scatter | solution.py:44
  176.1 2.1 fusion.6
  178.4 4.2 %fusion.52 = (bf16[192,1024]{1,0:T(8,128)(2,1)S(1)}, f32[192,1024]{1,0:T(8,128)S(1)}) fusion(bf16[1024,2048]{1,0:T(8,128)(2,1)} %param.16, f32[192,2048]{1,0:T(8,128)} %scatter_custom_fusion), kind=kOutput, calls=%fused_computation.87 | convolution fusion | flops 805896192 | bytes 6946816 | tf_op jit(solution)/shard_map/dot_general | solution.py:70
  182.7 3.7 %collective-permute-start.2 = (bf16[32,1024]{1,0:T(8,128)(2,1)S(1)}, bf16[32,1024]{1,0:T(8,128)(2,1)S(1)}, u32[]{:S(2)}, u32[]{:S(2)}) collective-permute-start(bf16[32,1024]{1,0:T(8,128)(2,1)S(1)} %get-tuple-element.34), channel_id=1, source_target_pairs={{0,4},{4,8},{8,12},{12,16},{16,20},{20,24},{24,28},{28,32},{32,36}... | collective-permute-start | bytes 196616 | tf_op jit(solution)/shard_map/ppermute | solution.py:39
  189.1 12.6 %reduce-scatter.6.cloned.1.call-done = f32[64,1024]{1,0:T(8,128)} async-done(((f32[256,1024]{1,0:T(8,128)}), f32[64,1024]{1,0:T(8,128)}) %reduce-scatter.6.cloned.1.call-update) | async-done | bytes 262160 | tf_op jit(solution)/shard_map/reduce_scatter | solution.py:44
  202.0 17.0 %reduce-scatter.8.cloned.1.call-done = f32[32,1024]{1,0:T(8,128)} async-done(((f32[64,1024]{1,0:T(8,128)}), f32[32,1024]{1,0:T(8,128)}) %reduce-scatter.8.cloned.1.call-update) | async-done | bytes 131088 | tf_op jit(solution)/shard_map/reduce_scatter | solution.py:44
  220.6 3.7 %all-to-all-start = ((bf16[4,8,1024]{2,1,0:T(8,128)(2,1)}), bf16[4,8,1024]{2,1,0:T(8,128)(2,1)S(1)}, u32[]{:S(2)}, u32[]{:S(2)}) async-start(bf16[4,8,1024]{2,1,0:T(8,128)(2,1)} %convert_bitcast_fusion.2), calls=%async_computation.3 | async-start | bytes 131072 | tf_op jit(solution)/shard_map/all_to_all | solution.py:56
  225.2 3.6 %all-to-all-done = bf16[4,8,1024]{2,1,0:T(8,128)(2,1)S(1)} async-done(((bf16[4,8,1024]{2,1,0:T(8,128)(2,1)}), bf16[4,8,1024]{2,1,0:T(8,128)(2,1)S(1)}, u32[]{:S(2)}, u32[]{:S(2)}) %all-to-all-start) | async-done | bytes 65568 | tf_op jit(solution)/shard_map/all_to_all | solution.py:56
  (82 shorter events, 19.5 us)
Async XLA Ops:
  7.2 12.2 %copy-start = (bf16[1024,1024]{1,0:T(8,128)(2,1)S(1)}, bf16[1024,1024]{1,0:T(8,128)(2,1)}, u32[]{:S(2)}) copy-start(bf16[1024,1024]{1,0:T(8,128)(2,1)} %param.17) | copy-start | bytes 6291460
  7.2 14.6 %copy-start.5 = (bf16[1,32,1024]{2,1,0:T(8,128)(2,1)S(1)}, bf16[1,32,1024]{2,1,0:T(8,128)(2,1)}, u32[]{:S(2)}) copy-start(bf16[1,32,1024]{2,1,0:T(8,128)(2,1)} %param.15) | copy-start | bytes 196612
  7.2 168.4 %reduce-scatter.4.cloned.1.call-start = ((), (), s32[]{:S(2)}) async-start(), calls=%async_computation.4 | async-start | bytes 9437184 | tf_op jit(solution)/shard_map/reduce_scatter | solution.py:44
  9.6 13.1 %copy-start.12 = (s32[32,12]{0,1:T(8,128)S(1)}, s32[32,12]{0,1:T(8,128)}, u32[]{:S(2)}) copy-start(s32[32,12]{0,1:T(8,128)} %param.21) | copy-start | bytes 4612
  9.6 13.1 %copy-start.11 = (s32[32,12]{0,1:T(8,128)S(1)}, s32[32,12]{0,1:T(8,128)}, u32[]{:S(2)}) copy-start(s32[32,12]{0,1:T(8,128)} %param.20) | copy-start | bytes 4612
  10.9 13.8 %collective-permute-start = (bf16[32,1024]{1,0:T(8,128)(2,1)S(1)}, bf16[32,1024]{1,0:T(8,128)(2,1)S(1)}, u32[]{:S(2)}, u32[]{:S(2)}) collective-permute-start(bf16[32,1024]{1,0:T(8,128)(2,1)S(1)} %get-tuple-element.35), channel_id=1, source_target_pairs={{0,4},{4,8},{8,12},{12,16},{16,20},{20,24},{24,28},{28,32},{32,36}... | collective-permute-start | bytes 196616 | tf_op jit(solution)/shard_map/ppermute | solution.py:27
  15.4 9.3 %collective-permute-start.1 = (bf16[32,1024]{1,0:T(8,128)(2,1)S(1)}, bf16[32,1024]{1,0:T(8,128)(2,1)S(1)}, u32[]{:S(2)}, u32[]{:S(2)}) collective-permute-start(bf16[32,1024]{1,0:T(8,128)(2,1)S(1)} %get-tuple-element.36), channel_id=1, source_target_pairs={{4,0},{8,4},{12,8},{16,12},{20,16},{24,20},{28,24},{32,28},{36,32}... | collective-permute-start | bytes 196616 | tf_op jit(solution)/shard_map/ppermute | solution.py:29
  24.7 3.3 %copy-start.6 = (bf16[32,1024]{1,0:T(8,128)(2,1)}, bf16[32,1024]{1,0:T(8,128)(2,1)S(1)}, u32[]{:S(2)}) copy-start(bf16[32,1024]{1,0:T(8,128)(2,1)S(1)} %collective-permute-done) | copy-start | bytes 196612
  24.7 3.2 %copy-start.8 = (bf16[32,1024]{1,0:T(8,128)(2,1)}, bf16[32,1024]{1,0:T(8,128)(2,1)S(1)}, u32[]{:S(2)}) copy-start(bf16[32,1024]{1,0:T(8,128)(2,1)S(1)} %collective-permute-done.1) | copy-start | bytes 196612
  47.4 3.4 %copy-start.3 = (f32[32,16,64]{2,1,0:T(8,128)S(1)}, f32[32,16,64]{2,1,0:T(8,128)}, u32[]{:S(2)}) copy-start(f32[32,16,64]{2,1,0:T(8,128)} %convert_element_type.82) | copy-start | bytes 393220
  53.0 3.8 %copy-start.2 = (f32[32,16,64]{2,1,0:T(8,128)S(1)}, f32[32,16,64]{2,1,0:T(8,128)}, u32[]{:S(2)}) copy-start(f32[32,16,64]{2,1,0:T(8,128)} %convert_element_type.80) | copy-start | bytes 393220
  62.6 8.2 %copy-start.7 = (bf16[32,1024]{1,0:T(8,128)(2,1)S(1)}, bf16[32,1024]{1,0:T(8,128)(2,1)}, u32[]{:S(2)}) copy-start(bf16[32,1024]{1,0:T(8,128)(2,1)} %copy-done.6) | copy-start | bytes 196612
  62.6 8.2 %copy-start.9 = (bf16[32,1024]{1,0:T(8,128)(2,1)S(1)}, bf16[32,1024]{1,0:T(8,128)(2,1)}, u32[]{:S(2)}) copy-start(bf16[32,1024]{1,0:T(8,128)(2,1)} %copy-done.8) | copy-start | bytes 196612
  76.7 124.9 %reduce-scatter.6.cloned.1.call-start = ((), (), s32[]{:S(2)}) async-start(), calls=%async_computation.5 | async-start | bytes 1310720 | tf_op jit(solution)/shard_map/reduce_scatter | solution.py:44
  175.7 43.4 %reduce-scatter.8.cloned.1.call-start = ((), (), s32[]{:S(2)}) async-start(), calls=%async_computation.6 | async-start | bytes 393216 | tf_op jit(solution)/shard_map/reduce_scatter | solution.py:44
  178.4 8.0 %copy-start.4 = (bf16[1,32,1024]{2,1,0:T(8,128)(2,1)S(1)}, bf16[1,32,1024]{2,1,0:T(8,128)(2,1)}, u32[]{:S(2)}) copy-start(bf16[1,32,1024]{2,1,0:T(8,128)(2,1)} %param.14) | copy-start | bytes 196612
  182.6 19.1 %copy-start.1 = (bf16[1,128,1024]{2,1,0:T(8,128)(2,1)S(1)}, bf16[1,128,1024]{2,1,0:T(8,128)(2,1)}, u32[]{:S(2)}) copy-start(bf16[1,128,1024]{2,1,0:T(8,128)(2,1)} %param.13) | copy-start | bytes 786436
  182.6 19.1 %copy-start.10 = (f32[1024]{0:T(1024)S(1)}, f32[1024]{0:T(1024)}, u32[]{:S(2)}) copy-start(f32[1024]{0:T(1024)} %param.18) | copy-start | bytes 12292
  182.7 6.4 %collective-permute-start.2 = (bf16[32,1024]{1,0:T(8,128)(2,1)S(1)}, bf16[32,1024]{1,0:T(8,128)(2,1)S(1)}, u32[]{:S(2)}, u32[]{:S(2)}) collective-permute-start(bf16[32,1024]{1,0:T(8,128)(2,1)S(1)} %get-tuple-element.34), channel_id=1, source_target_pairs={{0,4},{4,8},{8,12},{12,16},{16,20},{20,24},{24,28},{28,32},{32,36}... | collective-permute-start | bytes 196616 | tf_op jit(solution)/shard_map/ppermute | solution.py:39
  187.1 14.7 %collective-permute-start.3 = (bf16[32,1024]{1,0:T(8,128)(2,1)S(1)}, bf16[32,1024]{1,0:T(8,128)(2,1)S(1)}, u32[]{:S(2)}, u32[]{:S(2)}) collective-permute-start(bf16[32,1024]{1,0:T(8,128)(2,1)S(1)} %get-tuple-element.33), channel_id=1, source_target_pairs={{4,0},{8,4},{12,8},{16,12},{20,16},{24,20},{28,24},{32,28},{36,32}... | collective-permute-start | bytes 196616 | tf_op jit(solution)/shard_map/ppermute | solution.py:39
  220.6 8.2 %all-to-all-start = ((bf16[4,8,1024]{2,1,0:T(8,128)(2,1)}), bf16[4,8,1024]{2,1,0:T(8,128)(2,1)S(1)}, u32[]{:S(2)}, u32[]{:S(2)}) async-start(bf16[4,8,1024]{2,1,0:T(8,128)(2,1)} %convert_bitcast_fusion.2), calls=%async_computation.3 | async-start | bytes 131072 | tf_op jit(solution)/shard_map/all_to_all | solution.py:56
Sparse Core Ops, SparseCore 0:
  76.9 98.7 reduce-scatter.3
  178.2 23.4 reduce-scatter.5
  204.3 14.6 reduce-scatter.7
where the time goes:
time: 237 us; the launch traced here: 236 us
  waiting for transfers between devices  132 us (56%)
  local copies, waits for them, and re-layouts  27.3 us (12%)
  other arithmetic  23.7 us (10%)
  matrix products  22.8 us (10%)
  starting transfers between devices  15.9 us (7%)
  between operations  14.1 us (6%)
    reduce_scatter x3, waiting for transfers between devices, own_rows(): running = lax.psum_scatter(running, axis, scatter_dimension=0, tiled=True)  128 us
    scatter-add x1, other arithmetic, node_block(): partial_value = jnp.zeros((kv_window.shape[0], 2 * features), jnp.float32...  8.17 us
    gather x2, local copies, waits for them, and re-layouts, node_block(): gathered = kv_window[local_rows]  6.71 us
    dot_general x1, matrix products, rows_product(): lax.dot_general(partial_rows, normed_rows, (((0,), (0,)), ((), ())), pref...  5.93 us
    ppermute x2, starting transfers between devices, passed_along(): return lax.ppermute(value, axis, pairs)  5.65 us
  transfers between devices with their start and end apart: 8, of which 4 were waited for; matrix products, arithmetic and copies ran while one was open for 7% of the time, Pallas kernels for 0%

commit v1 on v0

v1 whole, which is shorter than its diff:
```python
import functools
import math

import jax
import jax.numpy as jnp
from jax import lax
from jax.experimental import pallas as pl
from jax.experimental.pallas import tpu as pltpu
from jax.sharding import Mesh
from jax.sharding import PartitionSpec as P

HEADS = 16
K = 12
R = 32
BAND = ("bz", "bx", "bc")
AXES = ("bz", "bx", "bc", "ens")
EPSILON = 1e-05
MESH = pl.DeviceIdType.MESH
F32 = jnp.float32
BF16 = jnp.bfloat16
LANES = 128


def dot(left, right, contract):
    return lax.dot_general(left, right, ((contract[:1], contract[1:]), ((), ())), preferred_element_type=F32)


def normalize(values):
    average = jnp.mean(values, axis=-1, keepdims=True)
    centred = values - average
    variance = jnp.mean(centred * centred, axis=-1, keepdims=True)
    inv_std = lax.rsqrt(variance + EPSILON)
    return centred * inv_std, inv_std


def layer_kernel(
    sizes,
    factor,
    grid_ref,
    hidden_ref,
    cot_ref,
    wkv_hbm,
    wq_hbm,
    src_gain_ref,
    q_gain_ref,
    index_ref,
    mask_ref,
    updated_ref,
    dgrid_ref,
    dw_ref,
    wkv,
    wq,
    standard,
    inv_std,
    win,
    pair_win,
    kv,
    partial,
    parted,
    pair_parted,
    d_norm,
    back_send,
    back_recv,
    send_a,
    recv_a,
    send_b,
    recv_b,
    send_a2,
    recv_a2,
    send_b2,
    recv_b2,
    kept,
    send_z,
    recv_z,
    load_sem,
    halo_send,
    halo_recv,
    pair_send,
    pair_recv,
    back_ssem,
    back_rsem,
    a_ssem,
    a_rsem,
    b_ssem,
    b_rsem,
    a2_ssem,
    a2_rsem,
    b2_ssem,
    b2_rsem,
    z_ssem,
    z_rsem,
):
    nz, nx, ny = sizes
    nb = nz * nx * 2
    rows = grid_ref.shape[0]
    nodes, features = hidden_ref.shape
    window = rows + 2 * R
    half = features // 2
    own = dw_ref.shape[0]

    z, x = lax.axis_index("bz"), lax.axis_index("bx")
    c, y = lax.axis_index("bc"), lax.axis_index("ens")
    band = (z * nx + x) * 2 + c

    def of_band(b):
        return (b // (2 * nx), (b // 2) % nx, b % 2, y)

    below = of_band((band + nb - 1) % nb)
    above = of_band((band + 1) % nb)
    pair = (z, x, 1 - c, y)

    def x_peer(k):
        return (z, (x + k) % nx, c, y)

    def y_peer(k):
        return (z, x, c, (y + k) % ny)

    def z_peer(k):
        return ((z + k) % nz, x, c, y)

    def remote(src, dst, ssem, rsem, device):
        return pltpu.make_async_remote_copy(
            src_ref=src, dst_ref=dst, send_sem=ssem, recv_sem=rsem, device_id=device, device_id_type=MESH
        )

    load_q = pltpu.make_async_copy(wq_hbm, wq, load_sem.at[0])
    load_kv = pltpu.make_async_copy(wkv_hbm, wkv, load_sem.at[1])
    load_q.start()
    load_kv.start()

    barrier = pltpu.get_barrier_semaphore()
    greeted = [below, above]
    greeted += [x_peer(k) for k in range(1, nx)]
    greeted += [y_peer(k) for k in range(1, ny)]
    greeted += [z_peer(k) for k in range(1, nz)]
    for device in greeted:
        pl.semaphore_signal(barrier, inc=1, device_id=device, device_id_type=MESH)

    hat, scale = normalize(grid_ref[...].astype(F32))
    standard[...] = hat
    inv_std[...] = scale
    win[R : R + rows] = (hat * src_gain_ref[...]).astype(BF16)

    pl.semaphore_wait(barrier, len(greeted))

    halo = [
        remote(win.at[R : 2 * R], win.at[R + rows : window], halo_send.at[0], halo_recv.at[0], below),
        remote(win.at[rows : rows + R], win.at[0:R], halo_send.at[1], halo_recv.at[1], above),
    ]
    for copy in halo:
        copy.start()

    hidden_hat, _ = normalize(hidden_ref[...].astype(F32))
    hidden_normed = (hidden_hat * q_gain_ref[...]).astype(BF16)
    load_q.wait()
    score_scale = 1.0 / math.sqrt(features // HEADS)
    queries = (dot(hidden_normed, wq[...], (1, 0)).astype(BF16).astype(F32) * score_scale).astype(BF16)

    local = index_ref[...] - (band * rows - R)
    local = jnp.where(mask_ref[...] > 0, local, -1)
    row_ids = lax.broadcasted_iota(jnp.int32, (nodes, window), 1)
    times = jnp.zeros((nodes, window), F32)
    for j in range(K):
        times = times + jnp.where(local[:, j : j + 1] == row_ids, 1.0, 0.0)
    times = jnp.concatenate([times, times], axis=0)
    live = times > 0.0

    load_kv.wait()
    for copy in halo:
        copy.wait_recv()
    swap_win = remote(win, pair_win, pair_send.at[0], pair_recv.at[0], pair)
    swap_win.start()
    for j in range(4):
        cols = pl.ds(j * half, half)
        kv[:, cols] = dot(win[...], wkv[:, cols], (1, 0)).astype(BF16)

    low_lane = lax.broadcasted_iota(jnp.int32, (nodes, LANES), 1) < features // HEADS
    cot = cot_ref[...]
    zero = jnp.zeros((nodes, LANES), F32)

    def two_heads(block):
        block = block.astype(F32)
        return jnp.concatenate(
            [jnp.where(low_lane, block, zero), jnp.where(low_lane, zero, block)], axis=0
        ).astype(BF16)

    group = ny * own

    def keep_parted(first, tile):
        piece = min(LANES, group)
        for i in range(LANES // piece):
            at, inside = divmod(first + i * piece, group)
            parted[at // (2 * nx), at // 2 % nx, at % 2, inside : inside + piece] = tile[i * piece : (i + 1) * piece]

    for j in range(features // LANES):
        span = slice(j * LANES, (j + 1) * LANES)
        vspan = slice(features + j * LANES, features + (j + 1) * LANES)
        q2 = two_heads(queries[:, span])
        d2 = two_heads(cot[:, span])
        k_rows, v_rows = kv[:, span], kv[:, vspan]
        scores = dot(q2, k_rows, (1, 1))
        d_probs = dot(d2, v_rows, (1, 1))
        shifted = jnp.where(live, scores, -jnp.inf)
        terms = jnp.exp(shifted - jnp.max(shifted, axis=1, keepdims=True))
        probs = terms / jnp.sum(times * terms, axis=1, keepdims=True)
        weights = (times * probs.astype(BF16).astype(F32)).astype(BF16)
        counted = times * probs
        d_scores = (counted * (d_probs - jnp.sum(counted * d_probs, axis=1, keepdims=True))).astype(BF16)
        mixed = dot(weights, v_rows, (1, 0))
        attended = jnp.where(low_lane, mixed[:nodes], mixed[nodes:])
        updated_ref[:, span] = (hidden_ref[:, span].astype(F32) + attended).astype(BF16)
        partial[:, span] = dot(d_scores, q2, (0, 0)).astype(BF16)
        partial[:, vspan] = dot(weights, d2, (0, 0)).astype(BF16)
        keep_parted(j * LANES, dot(q2, d_scores, (0, 0)).astype(BF16))
        keep_parted(features + j * LANES, dot(d2, weights, (0, 0)).astype(BF16))

    swap_part = remote(parted.at[:, :, 1 - c], pair_parted, pair_send.at[1], pair_recv.at[1], pair)
    swap_part.start()
    swap_win.wait()
    swap_part.wait()

    def product(xd, cols):
        mine = jnp.concatenate([parted[i, xd, c] for i in range(nz)], axis=0)
        other = jnp.concatenate([pair_parted[i, xd] for i in range(nz)], axis=0)
        return dot(mine, win[:, cols], (1, 0)) + dot(other, pair_win[:, cols], (1, 0))

    for xd in range(nx):
        tile = product(xd, slice(half, features)).reshape(nz, ny, own, half).astype(BF16)
        for yd in range(ny):
            send_b[yd, :, xd] = tile[:, yd]
    first_b = []
    for k in range(1, ny):
        first_b.append(remote(send_b.at[(y + k) % ny], recv_b.at[k - 1], b_ssem.at[k - 1], b_rsem.at[k - 1], y_peer(k)))
        first_b[-1].start()
    first_a = []
    for k in list(range(1, nx)) + [0]:
        tile = product((x + k) % nx, slice(0, half)).reshape(nz, ny, own, half).astype(BF16)
        send_a[k] = tile
        if k:
            first_a.append(remote(send_a.at[k], recv_a.at[k - 1], a_ssem.at[k - 1], a_rsem.at[k - 1], x_peer(k)))
            first_a[-1].start()

    part = partial[...]
    for j in range(2):
        cols = pl.ds(j * half, half)
        d_norm[:, cols] = dot(part, wkv[cols, :], (1, 1))
    back_send[0] = d_norm[0:R].astype(BF16)
    back_send[1] = d_norm[R + rows : window].astype(BF16)
    back = [
        remote(back_send.at[0], back_recv.at[0], back_ssem.at[0], back_rsem.at[0], below),
        remote(back_send.at[1], back_recv.at[1], back_ssem.at[1], back_rsem.at[1], above),
    ]
    for copy in back:
        copy.start()
    for copy in back:
        copy.wait()
    d_norm[R : 2 * R] += back_recv[1].astype(F32)
    d_norm[rows : rows + R] += back_recv[0].astype(F32)
    dx = d_norm[R : R + rows] * src_gain_ref[...]
    hat = standard[...]
    dgrid_ref[...] = (
        inv_std[...]
        * (dx - jnp.mean(dx, axis=-1, keepdims=True) - hat * jnp.mean(dx * hat, axis=-1, keepdims=True))
    ).astype(BF16)

    for copy in first_b:
        copy.wait()
    second_b = []
    for k in list(range(1, nx)) + [0]:
        xd = (x + k) % nx
        total = send_b[y, :, xd].astype(F32)
        for j in range(ny - 1):
            total = total + recv_b[j, :, xd].astype(F32)
        if k:
            send_b2[k - 1] = total.astype(BF16)
            second_b.append(
                remote(send_b2.at[k - 1], recv_b2.at[k - 1], b2_ssem.at[k - 1], b2_rsem.at[k - 1], x_peer(k))
            )
            second_b[-1].start()
        else:
            kept[:, :, half:] = total
    for copy in first_a:
        copy.wait()
    second_a = []
    for k in list(range(1, ny)) + [0]:
        yd = (y + k) % ny
        total = send_a[0, :, yd].astype(F32)
        for j in range(nx - 1):
            total = total + recv_a[j, :, yd].astype(F32)
        if k:
            send_a2[k - 1] = total.astype(BF16)
            second_a.append(
                remote(send_a2.at[k - 1], recv_a2.at[k - 1], a2_ssem.at[k - 1], a2_rsem.at[k - 1], y_peer(k))
            )
            second_a[-1].start()
        else:
            kept[:, :, :half] = total
    for copy in second_b:
        copy.wait()
    total = kept[:, :, half:]
    for j in range(nx - 1):
        total = total + recv_b2[j].astype(F32)
    send_z[:, :, half:] = total.astype(BF16)
    for copy in second_a:
        copy.wait()
    total = kept[:, :, :half]
    for j in range(ny - 1):
        total = total + recv_a2[j].astype(F32)
    send_z[:, :, :half] = total.astype(BF16)

    third = []
    for k in range(1, nz):
        third.append(
            remote(send_z.at[(z + k) % nz], recv_z.at[k - 1], z_ssem.at[k - 1], z_rsem.at[k - 1], z_peer(k))
        )
        third[-1].start()
    total = send_z[z].astype(F32)
    for k in range(1, nz):
        third[k - 1].wait()
        total = total + recv_z[k - 1].astype(F32)
    dw_ref[...] = total * factor
    for copy in halo:
        copy.wait_send()


def per_device(sizes, grid_latent, hidden, d_updated, w_kv, w_q, src_gain, q_gain, src_index, edge_mask):
    nz, nx, ny = sizes
    _, rows, features = grid_latent.shape
    nodes = hidden.shape[1]
    window = rows + 2 * R
    half = features // 2
    columns = w_kv.shape[1]
    own = columns // (nz * nx * 2 * ny)
    factor = 1.0 / math.sqrt(ny * rows * nz * nx * 2)
    vmem = pl.BlockSpec(memory_space=pltpu.VMEM)
    anywhere = pl.BlockSpec(memory_space=pl.ANY)
    dma = pltpu.SemaphoreType.DMA
    V = pltpu.VMEM
    scratch = [
        V((features, columns), BF16),
        V((features, features), BF16),
        V((rows, features), F32),
        V((rows, 1), F32),
        V((window, features), BF16),
        V((window, features), BF16),
        V((window, columns), BF16),
        V((window, columns), BF16),
        V((nz, nx, 2, ny * own, window), BF16),
        V((nz, nx, ny * own, window), BF16),
        V((window, features), F32),
        V((2, R, features), BF16),
        V((2, R, features), BF16),
        V((nx, nz, ny, own, half), BF16),
        V((nx - 1, nz, ny, own, half), BF16),
        V((ny, nz, nx, own, half), BF16),
        V((ny - 1, nz, nx, own, half), BF16),
        V((ny - 1, nz, own, half), BF16),
        V((ny - 1, nz, own, half), BF16),
        V((nx - 1, nz, own, half), BF16),
        V((nx - 1, nz, own, half), BF16),
        V((nz, own, features), F32),
        V((nz, own, features), BF16),
        V((nz - 1, own, features), BF16),
        dma((2,)),
        dma((2,)),
        dma((2,)),
        dma((2,)),
        dma((2,)),
        dma((2,)),
        dma((2,)),
        dma((nx - 1,)),
        dma((nx - 1,)),
        dma((ny - 1,)),
        dma((ny - 1,)),
        dma((ny - 1,)),
        dma((ny - 1,)),
        dma((nx - 1,)),
        dma((nx - 1,)),
        dma((nz - 1,)),
        dma((nz - 1,)),
    ]
    updated, d_grid, d_wkv_t = pl.pallas_call(
        functools.partial(layer_kernel, sizes, factor),
        out_shape=(
            jax.ShapeDtypeStruct((nodes, features), BF16),
            jax.ShapeDtypeStruct((rows, features), BF16),
            jax.ShapeDtypeStruct((own, features), F32),
        ),
        in_specs=[vmem, vmem, vmem, anywhere, anywhere, vmem, vmem, vmem, vmem],
        out_specs=(vmem, vmem, vmem),
        scratch_shapes=scratch,
        compiler_params=pltpu.CompilerParams(
            collective_id=0, has_side_effects=True, vmem_limit_bytes=52 * 1024 * 1024
        ),
        name="encoder_layer",
    )(
        grid_latent[0],
        hidden[0],
        d_updated[0],
        w_kv,
        w_q,
        src_gain.reshape(1, features),
        q_gain.reshape(1, features),
        src_index,
        edge_mask,
    )
    return (updated[None], d_grid[None], d_wkv_t)


def solution(mesh):
    bands, members = mesh.shape["band"], mesh.shape["ens"]
    nx = 4 if bands >= 64 else 2
    nz = bands // (2 * nx)
    finer = Mesh(mesh.devices.reshape(nz, nx, 2, members), AXES)
    cells = P("ens", BAND, None)
    in_specs = (cells, cells, cells, P(), P(), P(), P(), P(BAND, None), P(BAND, None))
    out_specs = (cells, cells, P(AXES, None))
    return jax.shard_map(
        functools.partial(per_device, (nz, nx, members)),
        mesh=finer,
        in_specs=in_specs,
        out_specs=out_specs,
        check_vma=False,
    )
```

time: 237 us -> 55 us (0.23)
  waiting for transfers between devices: 132 us -> 0 us
  Pallas kernels: 0 us -> 45.8 us
  other arithmetic: 23.7 us -> 0 us
  matrix products: 22.8 us -> 0 us
  local copies, waits for them, and re-layouts: 27.3 us -> 7.5 us
  starting transfers between devices: 15.9 us -> 0 us
  between operations: 14.1 us -> 0.65 us
    reduce_scatter x3 -> x0, waiting for transfers between devices: 128 us -> none  [own_rows(): running = lax.psum_scatter(running, axis, scatter_dimension=0, tiled=True)]
    pallas_call x0 -> x1, Pallas kernels: none -> 45.8 us  [per_device(): pl.pallas_call(functools.partial(layer_kernel, sizes, factor), out_shape=...]
    dot_general x7 -> x0, matrix products: 22.8 us -> none  [the longest x1 5.93 us: rows_product(): lax.dot_general(partial_rows, normed_rows, (((0,), (0,)), ((), ())), pref...]
    ppermute x4 -> x0, starting transfers between devices: 12.1 us -> none  [the longest x2 5.65 us: passed_along(): return lax.ppermute(value, axis, pairs)]
    scatter-add x3 -> x0, other arithmetic: 8.21 us -> none  [the longest x1 8.17 us: node_block(): partial_value = jnp.zeros((kv_window.shape[0], 2 * features), jnp.float32...]
    mul x3 -> x0, local copies, waits for them, and re-layouts: 7.62 us -> none  [the longest x1 3.75 us: node_block(): probs_low.astype(jnp.float32)[..., None]]
    unnamed x26 -> x15, local copies, waits for them, and re-layouts: 0.07 us -> 7.5 us
    reshape x6 -> x0, local copies, waits for them, and re-layouts: 6.83 us -> none  [the longest x1 3.6 us: node_block(): gathered[..., features:].reshape(node_count, K, HEADS, head_dim)]
  transfers between devices with their start and end apart: 8 -> 0, of which waited for: 4 -> 0; matrix products, arithmetic and copies ran while one was open for 7% -> 0% of each run, Pallas kernels for 0% -> 0%
where the time goes in v1:
time: 55 us; the launch traced here: 53.9 us
  Pallas kernels  45.8 us (83%)
  local copies, waits for them, and re-layouts  7.5 us (14%)
  between operations  0.65 us (1%)
    pallas_call x1, Pallas kernels, per_device(): pl.pallas_call(functools.partial(layer_kernel, sizes, factor), out_shape=...  45.8 us
    unnamed x15, local copies, waits for them, and re-layouts  7.5 us

profile of v1, /device:TPU:1, one launch (start us, length us, event | category | flops | bytes accessed | tf_op | source)
XLA Modules:
  0.0 53.9 jit_solution(11042639782895068989)
XLA Ops:
  0.6 0.8 %copy.12.index_ref = s32[32,12]{1,0:T(8,128)S(1)} copy(s32[32,12]{0,1:T(8,128)} %param.16) | data formatting | bytes 3072 | tf_op args[7]
  1.4 0.8 %copy.13.mask_ref = s32[32,12]{1,0:T(8,128)S(1)} copy(s32[32,12]{0,1:T(8,128)} %param.17) | data formatting | bytes 3072 | tf_op args[8]
  2.2 0.0 copy-start
  2.2 0.9 %copy-done = bf16[1,128,1024]{2,1,0:T(8,128)(2,1)S(1)} copy-done((bf16[1,128,1024]{2,1,0:T(8,128)(2,1)S(1)}, bf16[1,128,1024]{2,1,0:T(8,128)(2,1)}, u32[]{:S(2)}) %copy-start) | copy-done | bytes 262168
  3.1 0.0 copy-start.1
  3.1 0.8 %copy-done.1 = bf16[1,32,1024]{2,1,0:T(8,128)(2,1)S(1)} copy-done((bf16[1,32,1024]{2,1,0:T(8,128)(2,1)S(1)}, bf16[1,32,1024]{2,1,0:T(8,128)(2,1)}, u32[]{:S(2)}) %copy-start.1) | copy-done | bytes 65560
  4.0 0.0 copy-start.2
  4.0 0.8 %copy-done.2 = bf16[1,32,1024]{2,1,0:T(8,128)(2,1)S(1)} copy-done((bf16[1,32,1024]{2,1,0:T(8,128)(2,1)S(1)}, bf16[1,32,1024]{2,1,0:T(8,128)(2,1)}, u32[]{:S(2)}) %copy-start.2) | copy-done | bytes 65560
  4.8 0.0 copy-start.3
  4.8 0.7 %copy-done.3 = f32[1024]{0:T(1024)S(1)} copy-done((f32[1024]{0:T(1024)S(1)}, f32[1024]{0:T(1024)}, u32[]{:S(2)}) %copy-start.3) | copy-done | bytes 4120
  5.5 0.0 copy-start.4
  5.5 0.7 %copy-done.4 = f32[1024]{0:T(1024)S(1)} copy-done((f32[1024]{0:T(1024)S(1)}, f32[1024]{0:T(1024)}, u32[]{:S(2)}) %copy-start.4) | copy-done | bytes 4120
  6.2 45.8 %encoder_layer.1 = (bf16[32,1024]{1,0:T(8,128)(2,1)S(1)}, bf16[128,1024]{1,0:T(8,128)(2,1)S(1)}, f32[8,1024]{1,0:T(8,128)S(1)}) custom-call(bf16[128,1024]{1,0:T(8,128)(2,1)S(1)} %bitcast.7, bf16[32,1024]{1,0:T(8,128)(2,1)S(1)} %bitcast.9, bf16[32,1024]{1,0:T(8,128)(2,1)S(1)} %bitcast.10, bf16[1024,2048]{1,0:T(8,128)(2,1)} %wkv_hbm.1, ...), custom_call_target="tpu_custom_call" | custom-call | tf_op jit(solution)/shard_map/encoder_layer/pallas_call | solution.py:382
  52.0 0.6 %copy.17 = bf16[1,32,1024]{2,1,0:T(8,128)(2,1)} copy(bf16[1,32,1024]{2,1,0:T(8,128)(2,1)S(1)} %bitcast.11) | data formatting | bytes 131072
  52.6 0.7 %copy.18 = bf16[1,128,1024]{2,1,0:T(8,128)(2,1)} copy(bf16[1,128,1024]{2,1,0:T(8,128)(2,1)S(1)} %bitcast.8) | data formatting | bytes 524288
  53.3 0.6 %copy.19 = f32[8,1024]{1,0:T(8,128)} copy(f32[8,1024]{1,0:T(8,128)S(1)} %get-tuple-element.14) | data formatting | bytes 65536
Async XLA Ops:
  2.2 0.9 %copy-start = (bf16[1,128,1024]{2,1,0:T(8,128)(2,1)S(1)}, bf16[1,128,1024]{2,1,0:T(8,128)(2,1)}, u32[]{:S(2)}) copy-start(bf16[1,128,1024]{2,1,0:T(8,128)(2,1)} %param.9) | copy-start | bytes 786436
  3.1 0.8 %copy-start.1 = (bf16[1,32,1024]{2,1,0:T(8,128)(2,1)S(1)}, bf16[1,32,1024]{2,1,0:T(8,128)(2,1)}, u32[]{:S(2)}) copy-start(bf16[1,32,1024]{2,1,0:T(8,128)(2,1)} %param.10) | copy-start | bytes 196612
  4.0 0.8 %copy-start.2 = (bf16[1,32,1024]{2,1,0:T(8,128)(2,1)S(1)}, bf16[1,32,1024]{2,1,0:T(8,128)(2,1)}, u32[]{:S(2)}) copy-start(bf16[1,32,1024]{2,1,0:T(8,128)(2,1)} %param.11) | copy-start | bytes 196612
  4.8 0.7 %copy-start.3 = (f32[1024]{0:T(1024)S(1)}, f32[1024]{0:T(1024)}, u32[]{:S(2)}) copy-start(f32[1024]{0:T(1024)} %param.14) | copy-start | bytes 12292
  5.5 0.7 %copy-start.4 = (f32[1024]{0:T(1024)S(1)}, f32[1024]{0:T(1024)}, u32[]{:S(2)}) copy-start(f32[1024]{0:T(1024)} %param.15) | copy-start | bytes 12292

commit v2 on v1

--- a/solution.py
+++ b/solution.py
@@ -36,18 +36,30 @@
 def layer_kernel(
     sizes,
     factor,
+    grid_hbm,
+    hidden_hbm,
+    cot_hbm,
+    wkv_hbm,
+    wq_hbm,
+    src_gain_hbm,
+    q_gain_hbm,
+    index_hbm,
+    mask_hbm,
+    updated_hbm,
+    dgrid_hbm,
+    dw_hbm,
+    updated_ref,
+    dgrid_ref,
+    dw_ref,
+    out_sem,
     grid_ref,
     hidden_ref,
     cot_ref,
-    wkv_hbm,
-    wq_hbm,
     src_gain_ref,
     q_gain_ref,
     index_ref,
     mask_ref,
-    updated_ref,
-    dgrid_ref,
-    dw_ref,
+    edge,
     wkv,
     wq,
     standard,
@@ -75,6 +87,8 @@
     load_sem,
     halo_send,
     halo_recv,
+    win_send,
+    win_recv,
     pair_send,
     pair_recv,
     back_ssem,
@@ -92,11 +106,11 @@
 ):
     nz, nx, ny = sizes
     nb = nz * nx * 2
-    rows = grid_ref.shape[0]
-    nodes, features = hidden_ref.shape
+    rows = grid_hbm.shape[0]
+    nodes, features = hidden_hbm.shape
     window = rows + 2 * R
     half = features // 2
-    own = dw_ref.shape[0]
+    own = dw_hbm.shape[0]
 
     z, x = lax.axis_index("bz"), lax.axis_index("bx")
     c, y = lax.axis_index("bc"), lax.axis_index("ens")
@@ -123,10 +137,21 @@
             src_ref=src, dst_ref=dst, send_sem=ssem, recv_sem=rsem, device_id=device, device_id_type=MESH
         )
 
-    load_q = pltpu.make_async_copy(wq_hbm, wq, load_sem.at[0])
-    load_kv = pltpu.make_async_copy(wkv_hbm, wkv, load_sem.at[1])
-    load_q.start()
-    load_kv.start()
+    def load(src, dst, i):
+        copy = pltpu.make_async_copy(src, dst, load_sem.at[i])
+        copy.start()
+        return copy
+
+    load_grid = load(grid_hbm, grid_ref, 0)
+    load_gain = load(src_gain_hbm, src_gain_ref, 1)
+    load_hidden = load(hidden_hbm, hidden_ref, 2)
+    load_q_gain = load(q_gain_hbm, q_gain_ref, 3)
+    load_q = load(wq_hbm, wq, 4)
+    load_index = load(index_hbm, index_ref, 5)
+    load_mask = load(mask_hbm, mask_ref, 6)
+    quarter = [slice(j * half, (j + 1) * half) for j in range(4)]
+    load_kv = [load(wkv_hbm.at[:, cols], wkv.at[:, cols], 8 + j) for j, cols in enumerate(quarter)]
+    load_cot = load(cot_hbm, cot_ref, 7)
 
     barrier = pltpu.get_barrier_semaphore()
     greeted = [below, above]
@@ -136,43 +161,58 @@
     for device in greeted:
         pl.semaphore_signal(barrier, inc=1, device_id=device, device_id_type=MESH)
 
+    pl.semaphore_wait(barrier, len(greeted))
+
+    halo = [
+        remote(grid_hbm.at[0:R], edge.at[1], halo_send.at[0], halo_recv.at[0], below),
+        remote(grid_hbm.at[rows - R : rows], edge.at[0], halo_send.at[1], halo_recv.at[1], above),
+    ]
+    for copy in halo:
+        copy.start()
+
+    load_grid.wait()
+    load_gain.wait()
     hat, scale = normalize(grid_ref[...].astype(F32))
     standard[...] = hat
     inv_std[...] = scale
     win[R : R + rows] = (hat * src_gain_ref[...]).astype(BF16)
 
-    pl.semaphore_wait(barrier, len(greeted))
-
-    halo = [
-        remote(win.at[R : 2 * R], win.at[R + rows : window], halo_send.at[0], halo_recv.at[0], below),
-        remote(win.at[rows : rows + R], win.at[0:R], halo_send.at[1], halo_recv.at[1], above),
-    ]
-    for copy in halo:
-        copy.start()
-
+    load_hidden.wait()
+    load_q_gain.wait()
     hidden_hat, _ = normalize(hidden_ref[...].astype(F32))
     hidden_normed = (hidden_hat * q_gain_ref[...]).astype(BF16)
     load_q.wait()
     score_scale = 1.0 / math.sqrt(features // HEADS)
     queries = (dot(hidden_normed, wq[...], (1, 0)).astype(BF16).astype(F32) * score_scale).astype(BF16)
 
+    load_index.wait()
+    load_mask.wait()
     local = index_ref[...] - (band * rows - R)
     local = jnp.where(mask_ref[...] > 0, local, -1)
-    row_ids = lax.broadcasted_iota(jnp.int32, (nodes, window), 1)
-    times = jnp.zeros((nodes, window), F32)
+    row_ids = lax.broadcasted_iota(jnp.int32, (window, nodes), 0)
+    times = jnp.zeros((window, nodes), F32)
     for j in range(K):
-        times = times + jnp.where(local[:, j : j + 1] == row_ids, 1.0, 0.0)
+        times = times + jnp.where(local[j : j + 1, :] == row_ids, 1.0, 0.0)
+    times = times.T
     times = jnp.concatenate([times, times], axis=0)
     live = times > 0.0
 
-    load_kv.wait()
+    for j, cols in enumerate(quarter):
+        load_kv[j].wait()
+        kv[R : R + rows, cols] = dot(win[R : R + rows], wkv[:, cols], (1, 0)).astype(BF16)
     for copy in halo:
         copy.wait_recv()
-    swap_win = remote(win, pair_win, pair_send.at[0], pair_recv.at[0], pair)
+    hat, _ = normalize(edge[...].reshape(2 * R, features).astype(F32))
+    outer = (hat * src_gain_ref[...]).astype(BF16)
+    win[0:R] = outer[:R]
+    win[R + rows : window] = outer[R:]
+    swap_win = remote(win, pair_win, win_send, win_recv, pair)
     swap_win.start()
-    for j in range(4):
-        cols = pl.ds(j * half, half)
-        kv[:, cols] = dot(win[...], wkv[:, cols], (1, 0)).astype(BF16)
+    for cols in quarter:
+        tile = dot(outer, wkv[:, cols], (1, 0)).astype(BF16)
+        kv[0:R, cols] = tile[:R]
+        kv[R + rows : window, cols] = tile[R:]
+    load_cot.wait()
 
     low_lane = lax.broadcasted_iota(jnp.int32, (nodes, LANES), 1) < features // HEADS
     cot = cot_ref[...]
@@ -186,13 +226,31 @@
 
     group = ny * own
 
+    swaps = []
+
     def keep_parted(first, tile):
         piece = min(LANES, group)
         for i in range(LANES // piece):
             at, inside = divmod(first + i * piece, group)
-            parted[at // (2 * nx), at // 2 % nx, at % 2, inside : inside + piece] = tile[i * piece : (i + 1) * piece]
-
-    for j in range(features // LANES):
+            parted[at % 2, at // (2 * nx), at // 2 % nx, inside : inside + piece, :window] = tile[i * piece : (i + 1) * piece]
+
+    def swap(first, count):
+        n = len(swaps)
+        swaps.append(
+            remote(
+                parted.at[1 - c, first : first + count],
+                pair_parted.at[first : first + count],
+                pair_send.at[n],
+                pair_recv.at[n],
+                pair,
+            )
+        )
+        swaps[-1].start()
+
+    batches = 2 if nz >= 4 else 1
+    blocks = features // LANES
+    planes = nz // (2 * batches)
+    for j in range(blocks):
         span = slice(j * LANES, (j + 1) * LANES)
         vspan = slice(features + j * LANES, features + (j + 1) * LANES)
         q2 = two_heads(queries[:, span])
@@ -213,32 +271,40 @@
         partial[:, vspan] = dot(weights, d2, (0, 0)).astype(BF16)
         keep_parted(j * LANES, dot(q2, d_scores, (0, 0)).astype(BF16))
         keep_parted(features + j * LANES, dot(d2, weights, (0, 0)).astype(BF16))
-
-    swap_part = remote(parted.at[:, :, 1 - c], pair_parted, pair_send.at[1], pair_recv.at[1], pair)
-    swap_part.start()
+        if (j + 1) % (blocks // batches) == 0:
+            batch = j * batches // blocks
+            swap(batch * planes, planes)
+            swap(nz // 2 + batch * planes, planes)
+
+    outs = [pltpu.make_async_copy(updated_ref, updated_hbm, out_sem.at[0])]
+    outs[0].start()
     swap_win.wait()
-    swap_part.wait()
+    for copy in swaps:
+        copy.wait()
 
     def product(xd, cols):
-        mine = jnp.concatenate([parted[i, xd, c] for i in range(nz)], axis=0)
-        other = jnp.concatenate([pair_parted[i, xd] for i in range(nz)], axis=0)
+        mine = jnp.concatenate([parted[c, i, xd, :, :window] for i in range(nz)], axis=0)
+        other = jnp.concatenate([pair_parted[i, xd, :, :window] for i in range(nz)], axis=0)
         return dot(mine, win[:, cols], (1, 0)) + dot(other, pair_win[:, cols], (1, 0))
 
+    first_a, first_b = [], []
+
+    def x_first(k):
+        send_a[k] = product((x + k) % nx, slice(0, half)).reshape(nz, ny, own, half).astype(BF16)
+        if k:
+            first_a.append(remote(send_a.at[k], recv_a.at[k - 1], a_ssem.at[k - 1], a_rsem.at[k - 1], x_peer(k)))
+            first_a[-1].start()
+
+    x_first(1)
     for xd in range(nx):
         tile = product(xd, slice(half, features)).reshape(nz, ny, own, half).astype(BF16)
         for yd in range(ny):
             send_b[yd, :, xd] = tile[:, yd]
-    first_b = []
     for k in range(1, ny):
         first_b.append(remote(send_b.at[(y + k) % ny], recv_b.at[k - 1], b_ssem.at[k - 1], b_rsem.at[k - 1], y_peer(k)))
         first_b[-1].start()
-    first_a = []
-    for k in list(range(1, nx)) + [0]:
-        tile = product((x + k) % nx, slice(0, half)).reshape(nz, ny, own, half).astype(BF16)
-        send_a[k] = tile
-        if k:
-            first_a.append(remote(send_a.at[k], recv_a.at[k - 1], a_ssem.at[k - 1], a_rsem.at[k - 1], x_peer(k)))
-            first_a[-1].start()
+    for k in list(range(2, nx)) + [0]:
+        x_first(k)
 
     part = partial[...]
     for j in range(2):
@@ -262,6 +328,9 @@
         inv_std[...]
         * (dx - jnp.mean(dx, axis=-1, keepdims=True) - hat * jnp.mean(dx * hat, axis=-1, keepdims=True))
     ).astype(BF16)
+
+    outs.append(pltpu.make_async_copy(dgrid_ref, dgrid_hbm, out_sem.at[1]))
+    outs[1].start()
 
     for copy in first_b:
         copy.wait()
@@ -319,8 +388,29 @@
         third[k - 1].wait()
         total = total + recv_z[k - 1].astype(F32)
     dw_ref[...] = total * factor
+    outs.append(pltpu.make_async_copy(dw_ref, dw_hbm, out_sem.at[2]))
+    outs[2].start()
+    for copy in outs:
+        copy.wait()
     for copy in halo:
         copy.wait_send()
+
+
+def leave_kernel(a, b, c, a_out, b_out, c_out, a_held, b_held, c_held, sem):
+    into = [
+        pltpu.make_async_copy(src, dst, sem.at[i]) for i, (src, dst) in enumerate([(b, b_held), (a, a_held), (c, c_held)])
+    ]
+    out = [
+        pltpu.make_async_copy(src, dst, sem.at[3 + i])
+        for i, (src, dst) in enumerate([(b_held, b_out), (a_held, a_out), (c_held, c_out)])
+    ]
+    for copy in into:
+        copy.start()
+    for first, second in zip(into, out):
+        first.wait()
+        second.start()
+    for copy in out:
+        copy.wait()
 
 
 def per_device(sizes, grid_latent, hidden, d_updated, w_kv, w_q, src_gain, q_gain, src_index, edge_mask):
@@ -333,10 +423,24 @@
     own = columns // (nz * nx * 2 * ny)
     factor = 1.0 / math.sqrt(ny * rows * nz * nx * 2)
     vmem = pl.BlockSpec(memory_space=pltpu.VMEM)
-    anywhere = pl.BlockSpec(memory_space=pl.ANY)
+    hbm = pl.BlockSpec(memory_space=pltpu.HBM)
     dma = pltpu.SemaphoreType.DMA
     V = pltpu.VMEM
+    padded = -(-window // LANES) * LANES
+    swaps = 4 if nz >= 4 else 2
     scratch = [
+        V((nodes, features), BF16),
+        V((rows, features), BF16),
+        V((own, features), F32),
+        dma((3,)),
+        V((rows, features), BF16),
+        V((nodes, features), BF16),
+        V((nodes, features), BF16),
+        V((1, features), F32),
+        V((1, features), F32),
+        V((K, nodes), jnp.int32),
+        V((K, nodes), jnp.int32),
+        V((2, R, features), BF16),
         V((features, columns), BF16),
         V((features, features), BF16),
         V((rows, features), F32),
@@ -345,8 +449,8 @@
         V((window, features), BF16),
         V((window, columns), BF16),
         V((window, columns), BF16),
-        V((nz, nx, 2, ny * own, window), BF16),
-        V((nz, nx, ny * own, window), BF16),
+        V((2, nz, nx, ny * own, padded), BF16),
+        V((nz, nx, ny * own, padded), BF16),
         V((window, features), F32),
         V((2, R, features), BF16),
         V((2, R, features), BF16),
@@ -361,11 +465,13 @@
         V((nz, own, features), F32),
         V((nz, own, features), BF16),
         V((nz - 1, own, features), BF16),
+        dma((12,)),
         dma((2,)),
         dma((2,)),
-        dma((2,)),
-        dma((2,)),
-        dma((2,)),
+        dma,
+        dma,
+        dma((swaps,)),
+        dma((swaps,)),
         dma((2,)),
         dma((2,)),
         dma((nx - 1,)),
@@ -386,11 +492,11 @@
             jax.ShapeDtypeStruct((rows, features), BF16),
             jax.ShapeDtypeStruct((own, features), F32),
         ),
-        in_specs=[vmem, vmem, vmem, anywhere, anywhere, vmem, vmem, vmem, vmem],
-        out_specs=(vmem, vmem, vmem),
+        in_specs=[hbm] * 9,
+        out_specs=(hbm, hbm, hbm),
         scratch_shapes=scratch,
         compiler_params=pltpu.CompilerParams(
-            collective_id=0, has_side_effects=True, vmem_limit_bytes=52 * 1024 * 1024
+            collective_id=0, has_side_effects=True, vmem_limit_bytes=60 * 1024 * 1024
         ),
         name="encoder_layer",
     )(
@@ -401,9 +507,27 @@
         w_q,
         src_gain.reshape(1, features),
         q_gain.reshape(1, features),
-        src_index,
-        edge_mask,
+        src_index.T,
+        edge_mask.T,
     )
+    updated, d_grid, d_wkv_t = pl.pallas_call(
+        leave_kernel,
+        out_shape=(
+            jax.ShapeDtypeStruct((nodes, features), BF16),
+            jax.ShapeDtypeStruct((rows, features), BF16),
+            jax.ShapeDtypeStruct((own, features), F32),
+        ),
+        in_specs=[hbm, hbm, hbm],
+        out_specs=(hbm, hbm, hbm),
+        scratch_shapes=[
+            V((nodes, features), BF16),
+            V((rows, features), BF16),
+            V((own, features), F32),
+            dma((6,)),
+        ],
+        compiler_params=pltpu.CompilerParams(vmem_limit_bytes=60 * 1024 * 1024),
+        name="leave",
+    )(updated, d_grid, d_wkv_t)
     return (updated[None], d_grid[None], d_wkv_t)
 
 

time: 55 us -> 49.8 us (0.905); the launches traced: 53.9 us -> 49.7 us
  local copies, waits for them, and re-layouts: 7.5 us -> 0 us
  Pallas kernels: 45.8 us -> 49.1 us
    unnamed x15 -> x0, local copies, waits for them, and re-layouts: 7.5 us -> none
    pallas_call x0 -> x1, Pallas kernels: none -> 1.72 us  [per_device(): pl.pallas_call(leave_kernel, out_shape=(jax.ShapeDtypeStruct((nodes, feat...]
    pallas_call x1, Pallas kernels: 45.8 us -> 47.3 us  [per_device(): pl.pallas_call(functools.partial(layer_kernel, sizes, factor), out_shape=...]
where the time goes in v2:
time: 49.8 us; the launch traced here: 49.7 us
  Pallas kernels  49.1 us (99%)
  between operations  0.64 us (1%)
    pallas_call x1, Pallas kernels, per_device(): pl.pallas_call(functools.partial(layer_kernel, sizes, factor), out_shape=...  47.3 us
    pallas_call x1, Pallas kernels, per_device(): pl.pallas_call(leave_kernel, out_shape=(jax.ShapeDtypeStruct((nodes, feat...  1.72 us

profile of v2, /device:TPU:1, one launch (start us, length us, event | category | flops | bytes accessed | tf_op | source)
XLA Modules:
  0.0 49.7 jit_solution(5009187903391456484)
XLA Ops:
  0.6 47.3 %encoder_layer.1 = (bf16[32,1024]{1,0:T(8,128)(2,1)}, bf16[128,1024]{1,0:T(8,128)(2,1)}, f32[8,1024]{1,0:T(8,128)}) custom-call(bf16[128,1024]{1,0:T(8,128)(2,1)} %bitcast.9, bf16[32,1024]{1,0:T(8,128)(2,1)} %bitcast.10, bf16[32,1024]{1,0:T(8,128)(2,1)} %bitcast.11, bf16[1024,2048]{1,0:T(8,128)(2,1)} %wkv_hbm.1, bf16[1024,1024]{1,0:T(8,128)(2,1)} %wq_hbm.1, ...), custom_call_target="tpu_custom_call" | custom-call | tf_op jit(solution)/shard_map/encoder_layer/pallas_call | solution.py:488
  48.0 1.7 %leave.1 = (bf16[32,1024]{1,0:T(8,128)(2,1)}, bf16[128,1024]{1,0:T(8,128)(2,1)}, f32[8,1024]{1,0:T(8,128)}) custom-call(bf16[32,1024]{1,0:T(8,128)(2,1)} %get-tuple-element.9.a, bf16[128,1024]{1,0:T(8,128)(2,1)} %get-tuple-element.10.b, f32[8,1024]{1,0:T(8,128)} %get-tuple-element.11.c), custom_call_target="tpu_custom_call" | custom-call | tf_op jit(solution)/shard_map/leave/pallas_call | solution.py:513

commit v3 on v2

--- a/solution.py
+++ b/solution.py
@@ -19,6 +19,7 @@
 F32 = jnp.float32
 BF16 = jnp.bfloat16
 LANES = 128
+WIDTHS = (256, 256)
 
 
 def dot(left, right, contract):
@@ -73,17 +74,7 @@
     d_norm,
     back_send,
     back_recv,
-    send_a,
-    recv_a,
-    send_b,
-    recv_b,
-    send_a2,
-    recv_a2,
-    send_b2,
-    recv_b2,
-    kept,
-    send_z,
-    recv_z,
+    lots,
     load_sem,
     halo_send,
     halo_recv,
@@ -93,16 +84,6 @@
     pair_recv,
     back_ssem,
     back_rsem,
-    a_ssem,
-    a_rsem,
-    b_ssem,
-    b_rsem,
-    a2_ssem,
-    a2_rsem,
-    b2_ssem,
-    b2_rsem,
-    z_ssem,
-    z_rsem,
 ):
     nz, nx, ny = sizes
     nb = nz * nx * 2
@@ -143,16 +124,6 @@
         return copy
 
     load_grid = load(grid_hbm, grid_ref, 0)
-    load_gain = load(src_gain_hbm, src_gain_ref, 1)
-    load_hidden = load(hidden_hbm, hidden_ref, 2)
-    load_q_gain = load(q_gain_hbm, q_gain_ref, 3)
-    load_q = load(wq_hbm, wq, 4)
-    load_index = load(index_hbm, index_ref, 5)
-    load_mask = load(mask_hbm, mask_ref, 6)
-    quarter = [slice(j * half, (j + 1) * half) for j in range(4)]
-    load_kv = [load(wkv_hbm.at[:, cols], wkv.at[:, cols], 8 + j) for j, cols in enumerate(quarter)]
-    load_cot = load(cot_hbm, cot_ref, 7)
-
     barrier = pltpu.get_barrier_semaphore()
     greeted = [below, above]
     greeted += [x_peer(k) for k in range(1, nx)]
@@ -161,16 +132,26 @@
     for device in greeted:
         pl.semaphore_signal(barrier, inc=1, device_id=device, device_id_type=MESH)
 
+    load_gain = load(src_gain_hbm, src_gain_ref, 1)
+    load_hidden = load(hidden_hbm, hidden_ref, 2)
+    load_q_gain = load(q_gain_hbm, q_gain_ref, 3)
+    load_index = load(index_hbm, index_ref, 5)
+    load_mask = load(mask_hbm, mask_ref, 6)
+    load_cot = load(cot_hbm, cot_ref, 7)
+    load_q = load(wq_hbm, wq, 4)
+    quarter = [slice(j * half, (j + 1) * half) for j in range(4)]
+    load_kv = [load(wkv_hbm.at[:, cols], wkv.at[:, cols], 8 + j) for j, cols in enumerate(quarter)]
+
+    load_grid.wait()
     pl.semaphore_wait(barrier, len(greeted))
 
     halo = [
-        remote(grid_hbm.at[0:R], edge.at[1], halo_send.at[0], halo_recv.at[0], below),
-        remote(grid_hbm.at[rows - R : rows], edge.at[0], halo_send.at[1], halo_recv.at[1], above),
+        remote(grid_ref.at[0:R], edge.at[1], halo_send.at[0], halo_recv.at[0], below),
+        remote(grid_ref.at[rows - R : rows], edge.at[0], halo_send.at[1], halo_recv.at[1], above),
     ]
     for copy in halo:
         copy.start()
 
-    load_grid.wait()
     load_gain.wait()
     hat, scale = normalize(grid_ref[...].astype(F32))
     standard[...] = hat
@@ -287,24 +268,71 @@
         other = jnp.concatenate([pair_parted[i, xd, :, :window] for i in range(nz)], axis=0)
         return dot(mine, win[:, cols], (1, 0)) + dot(other, pair_win[:, cols], (1, 0))
 
-    first_a, first_b = [], []
-
-    def x_first(k):
-        send_a[k] = product((x + k) % nx, slice(0, half)).reshape(nz, ny, own, half).astype(BF16)
-        if k:
-            first_a.append(remote(send_a.at[k], recv_a.at[k - 1], a_ssem.at[k - 1], a_rsem.at[k - 1], x_peer(k)))
-            first_a[-1].start()
-
-    x_first(1)
-    for xd in range(nx):
-        tile = product(xd, slice(half, features)).reshape(nz, ny, own, half).astype(BF16)
-        for yd in range(ny):
-            send_b[yd, :, xd] = tile[:, yd]
-    for k in range(1, ny):
-        first_b.append(remote(send_b.at[(y + k) % ny], recv_b.at[k - 1], b_ssem.at[k - 1], b_rsem.at[k - 1], y_peer(k)))
-        first_b[-1].start()
-    for k in list(range(2, nx)) + [0]:
-        x_first(k)
+    starts = []
+    left = 0
+    for lot in lots:
+        starts.append(left)
+        left += lot["kept_a"].shape[-1]
+    low, high = slice(0, nz // 2), slice(nz // 2, nz)
+
+    def neighbours(lot, name, peer, piece):
+        held, ssem, rsem = lot["recv_" + name], lot["ssem_" + name], lot["rsem_" + name]
+
+        def forward(lot):
+            over = lot["over_" + name]
+            copies = [
+                remote(piece(2).at[low], over.at[0], ssem.at[0], rsem.at[0], peer(1)),
+                remote(piece(2).at[high], over.at[1], ssem.at[1], rsem.at[1], peer(3)),
+            ]
+            for copy in copies:
+                copy.start()
+            return copies
+
+        def direct(k):
+            i, part = (0, high) if k == 1 else (1, low)
+            copy = remote(piece(k).at[part], held.at[i, part], ssem.at[2 + i], rsem.at[2 + i], peer(k))
+            copy.start()
+            return [copy]
+
+        def augment(lot, forwards):
+            over, copies = lot["over_" + name], []
+            for i, (k, part) in enumerate([(1, low), (3, high)]):
+                forwards[i].wait()
+                target = piece(k).at[part]
+                target[...] = (target[...].astype(F32) + over[i].astype(F32)).astype(BF16)
+                copies.append(remote(target, held.at[i, part], ssem.at[4 + i], rsem.at[4 + i], peer(k)))
+                copies[-1].start()
+            return copies
+
+        return forward, direct, augment
+
+    first, augments = [], []
+    for lot, start in zip(lots, starts):
+        width = lot["kept_a"].shape[-1]
+        send_a, send_b = lot["send_a"], lot["send_b"]
+        forward_a, direct_a, augment_a = neighbours(lot, "a", x_peer, lambda k, ref=send_a: ref.at[k])
+        forward_b, direct_b, augment_b = neighbours(lot, "b", y_peer, lambda k, ref=send_b: ref.at[(y + k) % ny])
+
+        def x_piece(k):
+            tile = product((x + k) % nx, slice(start, start + width))
+            send_a[k] = tile.reshape(nz, ny, own, width).astype(BF16)
+
+        x_piece(2)
+        over_a = forward_a(lot)
+        for xd in range(nx):
+            tile = product(xd, slice(half + start, half + start + width))
+            tile = tile.reshape(nz, ny, own, width).astype(BF16)
+            for yd in range(ny):
+                send_b[yd, :, xd] = tile[:, yd]
+        over_b = forward_b(lot)
+        copies_b = direct_b(1) + direct_b(3)
+        x_piece(1)
+        copies_a = direct_a(1)
+        x_piece(3)
+        copies_a += direct_a(3)
+        x_piece(0)
+        first.append((copies_a, copies_b))
+        augments.append((augment_a, augment_b, over_a, over_b))
 
     part = partial[...]
     for j in range(2):
@@ -318,6 +346,67 @@
     ]
     for copy in back:
         copy.start()
+    def second_exchange(lot, copies_a, copies_b):
+        sent_a, sent_b = [], []
+        for copy in copies_b:
+            copy.wait()
+        for k in list(range(1, nx)) + [0]:
+            xd = (x + k) % nx
+            total = lot["send_b"][y, :, xd].astype(F32)
+            for j in range(2):
+                total = total + lot["recv_b"][j, :, xd].astype(F32)
+            if k:
+                i = k - 1
+                lot["send_b2"][i] = total.astype(BF16)
+                src, dst = lot["send_b2"].at[i], lot["recv_b2"].at[i]
+                sent_b.append(remote(src, dst, lot["b2_ssem"].at[i], lot["b2_rsem"].at[i], x_peer(k)))
+                sent_b[-1].start()
+            else:
+                lot["kept_b"][...] = total
+        for copy in copies_a:
+            copy.wait()
+        for k in list(range(1, ny)) + [0]:
+            yd = (y + k) % ny
+            total = lot["send_a"][0, :, yd].astype(F32)
+            for j in range(2):
+                total = total + lot["recv_a"][j, :, yd].astype(F32)
+            if k:
+                i = k - 1
+                lot["send_a2"][i] = total.astype(BF16)
+                src, dst = lot["send_a2"].at[i], lot["recv_a2"].at[i]
+                sent_a.append(remote(src, dst, lot["a2_ssem"].at[i], lot["a2_rsem"].at[i], y_peer(k)))
+                sent_a[-1].start()
+            else:
+                lot["kept_a"][...] = total
+        return sent_a, sent_b
+
+    def third_exchange(lot, copies_a, copies_b):
+        width = lot["kept_a"].shape[-1]
+        send, sent = lot["send_z"], []
+        for copy in copies_b:
+            copy.wait()
+        total = lot["kept_b"][...]
+        for j in range(nx - 1):
+            total = total + lot["recv_b2"][j].astype(F32)
+        send[:, :, width:] = total.astype(BF16)
+        for copy in copies_a:
+            copy.wait()
+        total = lot["kept_a"][...]
+        for j in range(ny - 1):
+            total = total + lot["recv_a2"][j].astype(F32)
+        send[:, :, :width] = total.astype(BF16)
+        for k in range(1, nz):
+            i, src = k - 1, send.at[(z + k) % nz]
+            sent.append(remote(src, lot["recv_z"].at[i], lot["z_ssem"].at[i], lot["z_rsem"].at[i], z_peer(k)))
+            sent[-1].start()
+        return sent
+
+    for lot, (augment_a, augment_b, over_a, over_b), (copies_a, copies_b) in zip(lots, augments, first):
+        copies_a += augment_a(lot, over_a)
+        copies_b += augment_b(lot, over_b)
+
+    second = [second_exchange(lots[0], *first[0])]
+
     for copy in back:
         copy.wait()
     d_norm[R : 2 * R] += back_recv[1].astype(F32)
@@ -332,62 +421,18 @@
     outs.append(pltpu.make_async_copy(dgrid_ref, dgrid_hbm, out_sem.at[1]))
     outs[1].start()
 
-    for copy in first_b:
-        copy.wait()
-    second_b = []
-    for k in list(range(1, nx)) + [0]:
-        xd = (x + k) % nx
-        total = send_b[y, :, xd].astype(F32)
-        for j in range(ny - 1):
-            total = total + recv_b[j, :, xd].astype(F32)
-        if k:
-            send_b2[k - 1] = total.astype(BF16)
-            second_b.append(
-                remote(send_b2.at[k - 1], recv_b2.at[k - 1], b2_ssem.at[k - 1], b2_rsem.at[k - 1], x_peer(k))
-            )
-            second_b[-1].start()
-        else:
-            kept[:, :, half:] = total
-    for copy in first_a:
-        copy.wait()
-    second_a = []
-    for k in list(range(1, ny)) + [0]:
-        yd = (y + k) % ny
-        total = send_a[0, :, yd].astype(F32)
-        for j in range(nx - 1):
-            total = total + recv_a[j, :, yd].astype(F32)
-        if k:
-            send_a2[k - 1] = total.astype(BF16)
-            second_a.append(
-                remote(send_a2.at[k - 1], recv_a2.at[k - 1], a2_ssem.at[k - 1], a2_rsem.at[k - 1], y_peer(k))
-            )
-            second_a[-1].start()
-        else:
-            kept[:, :, :half] = total
-    for copy in second_b:
-        copy.wait()
-    total = kept[:, :, half:]
-    for j in range(nx - 1):
-        total = total + recv_b2[j].astype(F32)
-    send_z[:, :, half:] = total.astype(BF16)
-    for copy in second_a:
-        copy.wait()
-    total = kept[:, :, :half]
-    for j in range(ny - 1):
-        total = total + recv_a2[j].astype(F32)
-    send_z[:, :, :half] = total.astype(BF16)
-
-    third = []
-    for k in range(1, nz):
-        third.append(
-            remote(send_z.at[(z + k) % nz], recv_z.at[k - 1], z_ssem.at[k - 1], z_rsem.at[k - 1], z_peer(k))
-        )
-        third[-1].start()
-    total = send_z[z].astype(F32)
-    for k in range(1, nz):
-        third[k - 1].wait()
-        total = total + recv_z[k - 1].astype(F32)
-    dw_ref[...] = total * factor
+    for lot, copies in zip(lots[1:], first[1:]):
+        second.append(second_exchange(lot, *copies))
+    third = [third_exchange(lot, *copies) for lot, copies in zip(lots, second)]
+    for lot, start, copies in zip(lots, starts, third):
+        width = lot["kept_a"].shape[-1]
+        total = lot["send_z"][z].astype(F32)
+        for k in range(1, nz):
+            copies[k - 1].wait()
+            total = total + lot["recv_z"][k - 1].astype(F32)
+        total = total * factor
+        dw_ref[:, start : start + width] = total[:, :width]
+        dw_ref[:, half + start : half + start + width] = total[:, width:]
     outs.append(pltpu.make_async_copy(dw_ref, dw_hbm, out_sem.at[2]))
     outs[2].start()
     for copy in outs:
@@ -428,6 +473,36 @@
     V = pltpu.VMEM
     padded = -(-window // LANES) * LANES
     swaps = 4 if nz >= 4 else 2
+    lots = []
+    for width in WIDTHS:
+        lots.append(
+            dict(
+                send_a=V((nx, nz, ny, own, width), BF16),
+                recv_a=V((2, nz, ny, own, width), BF16),
+                over_a=V((2, nz // 2, ny, own, width), BF16),
+                send_b=V((ny, nz, nx, own, width), BF16),
+                recv_b=V((2, nz, nx, own, width), BF16),
+                over_b=V((2, nz // 2, nx, own, width), BF16),
+                send_a2=V((ny - 1, nz, own, width), BF16),
+                recv_a2=V((ny - 1, nz, own, width), BF16),
+                send_b2=V((nx - 1, nz, own, width), BF16),
+                recv_b2=V((nx - 1, nz, own, width), BF16),
+                kept_a=V((nz, own, width), F32),
+                kept_b=V((nz, own, width), F32),
+                send_z=V((nz, own, 2 * width), BF16),
+                recv_z=V((nz - 1, own, 2 * width), BF16),
+                ssem_a=dma((6,)),
+                rsem_a=dma((6,)),
+                ssem_b=dma((6,)),
+                rsem_b=dma((6,)),
+                a2_ssem=dma((ny - 1,)),
+                a2_rsem=dma((ny - 1,)),
+                b2_ssem=dma((nx - 1,)),
+                b2_rsem=dma((nx - 1,)),
+                z_ssem=dma((nz - 1,)),
+                z_rsem=dma((nz - 1,)),
+            )
+        )
     scratch = [
         V((nodes, features), BF16),
         V((rows, features), BF16),
@@ -454,17 +529,7 @@
         V((window, features), F32),
         V((2, R, features), BF16),
         V((2, R, features), BF16),
-        V((nx, nz, ny, own, half), BF16),
-        V((nx - 1, nz, ny, own, half), BF16),
-        V((ny, nz, nx, own, half), BF16),
-        V((ny - 1, nz, nx, own, half), BF16),
-        V((ny - 1, nz, own, half), BF16),
-        V((ny - 1, nz, own, half), BF16),
-        V((nx - 1, nz, own, half), BF16),
-        V((nx - 1, nz, own, half), BF16),
-        V((nz, own, features), F32),
-        V((nz, own, features), BF16),
-        V((nz - 1, own, features), BF16),
+        lots,
         dma((12,)),
         dma((2,)),
         dma((2,)),
@@ -474,16 +539,6 @@
         dma((swaps,)),
         dma((2,)),
         dma((2,)),
-        dma((nx - 1,)),
-        dma((nx - 1,)),
-        dma((ny - 1,)),
-        dma((ny - 1,)),
-        dma((ny - 1,)),
-        dma((ny - 1,)),
-        dma((nx - 1,)),
-        dma((nx - 1,)),
-        dma((nz - 1,)),
-        dma((nz - 1,)),
     ]
     updated, d_grid, d_wkv_t = pl.pallas_call(
         functools.partial(layer_kernel, sizes, factor),
@@ -533,7 +588,7 @@
 
 def solution(mesh):
     bands, members = mesh.shape["band"], mesh.shape["ens"]
-    nx = 4 if bands >= 64 else 2
+    nx = 4
     nz = bands // (2 * nx)
     finer = Mesh(mesh.devices.reshape(nz, nx, 2, members), AXES)
     cells = P("ens", BAND, None)

time: 49.8 us -> 46 us (0.924); the launches traced: 49.7 us -> 45.1 us
  Pallas kernels: 49.1 us -> 44.4 us
    pallas_call x1, Pallas kernels: 47.3 us -> 42.7 us  [per_device(): pl.pallas_call(functools.partial(layer_kernel, sizes, factor), out_shape=...]
where the time goes in v3:
time: 46 us; the launch traced here: 45.1 us
  Pallas kernels  44.4 us (97%)
  between operations  0.64 us (1%)
    pallas_call x1, Pallas kernels, per_device(): pl.pallas_call(functools.partial(layer_kernel, sizes, factor), out_shape=...  42.7 us
    pallas_call x1, Pallas kernels, per_device(): pl.pallas_call(leave_kernel, out_shape=(jax.ShapeDtypeStruct((nodes, feat...  1.72 us

profile of v3, /device:TPU:1, one launch (start us, length us, event | category | flops | bytes accessed | tf_op | source)
XLA Modules:
  0.0 45.1 jit_solution(11987965457659773923)
XLA Ops:
  0.6 42.7 %encoder_layer.1 = (bf16[32,1024]{1,0:T(8,128)(2,1)}, bf16[128,1024]{1,0:T(8,128)(2,1)}, f32[8,1024]{1,0:T(8,128)}) custom-call(bf16[128,1024]{1,0:T(8,128)(2,1)} %bitcast.9, bf16[32,1024]{1,0:T(8,128)(2,1)} %bitcast.10, bf16[32,1024]{1,0:T(8,128)(2,1)} %bitcast.11, bf16[1024,2048]{1,0:T(8,128)(2,1)} %wkv_hbm.1, bf16[1024,1024]{1,0:T(8,128)(2,1)} %wq_hbm.1, ...), custom_call_target="tpu_custom_call" | custom-call | tf_op jit(solution)/shard_map/encoder_layer/pallas_call | solution.py:543
  43.3 1.7 %leave.1 = (bf16[32,1024]{1,0:T(8,128)(2,1)}, bf16[128,1024]{1,0:T(8,128)(2,1)}, f32[8,1024]{1,0:T(8,128)}) custom-call(bf16[32,1024]{1,0:T(8,128)(2,1)} %get-tuple-element.9.a, bf16[128,1024]{1,0:T(8,128)(2,1)} %get-tuple-element.10.b, f32[8,1024]{1,0:T(8,128)} %get-tuple-element.11.c), custom_call_target="tpu_custom_call" | custom-call | tf_op jit(solution)/shard_map/leave/pallas_call | solution.py:568

commit v4 on v3

--- a/solution.py
+++ b/solution.py
@@ -231,31 +231,35 @@
     batches = 2 if nz >= 4 else 1
     blocks = features // LANES
     planes = nz // (2 * batches)
-    for j in range(blocks):
-        span = slice(j * LANES, (j + 1) * LANES)
-        vspan = slice(features + j * LANES, features + (j + 1) * LANES)
-        q2 = two_heads(queries[:, span])
-        d2 = two_heads(cot[:, span])
-        k_rows, v_rows = kv[:, span], kv[:, vspan]
-        scores = dot(q2, k_rows, (1, 1))
-        d_probs = dot(d2, v_rows, (1, 1))
-        shifted = jnp.where(live, scores, -jnp.inf)
-        terms = jnp.exp(shifted - jnp.max(shifted, axis=1, keepdims=True))
-        probs = terms / jnp.sum(times * terms, axis=1, keepdims=True)
-        weights = (times * probs.astype(BF16).astype(F32)).astype(BF16)
-        counted = times * probs
-        d_scores = (counted * (d_probs - jnp.sum(counted * d_probs, axis=1, keepdims=True))).astype(BF16)
-        mixed = dot(weights, v_rows, (1, 0))
-        attended = jnp.where(low_lane, mixed[:nodes], mixed[nodes:])
-        updated_ref[:, span] = (hidden_ref[:, span].astype(F32) + attended).astype(BF16)
-        partial[:, span] = dot(d_scores, q2, (0, 0)).astype(BF16)
-        partial[:, vspan] = dot(weights, d2, (0, 0)).astype(BF16)
-        keep_parted(j * LANES, dot(q2, d_scores, (0, 0)).astype(BF16))
-        keep_parted(features + j * LANES, dot(d2, weights, (0, 0)).astype(BF16))
-        if (j + 1) % (blocks // batches) == 0:
-            batch = j * batches // blocks
-            swap(batch * planes, planes)
-            swap(nz // 2 + batch * planes, planes)
+    def spans(j):
+        return slice(j * LANES, (j + 1) * LANES), slice(features + j * LANES, features + (j + 1) * LANES)
+
+    for batch in range(batches):
+        mine = range(batch * blocks // batches, (batch + 1) * blocks // batches)
+        q2s = [two_heads(queries[:, spans(j)[0]]) for j in mine]
+        d2s = [two_heads(cot[:, spans(j)[0]]) for j in mine]
+        scores = [dot(q2, kv[:, spans(j)[0]], (1, 1)) for q2, j in zip(q2s, mine)]
+        d_probs = [dot(d2, kv[:, spans(j)[1]], (1, 1)) for d2, j in zip(d2s, mine)]
+        weights, d_scores = [], []
+        for score, d_prob in zip(scores, d_probs):
+            shifted = jnp.where(live, score, -jnp.inf)
+            terms = jnp.exp(shifted - jnp.max(shifted, axis=1, keepdims=True))
+            probs = terms / jnp.sum(times * terms, axis=1, keepdims=True)
+            weights.append((times * probs.astype(BF16).astype(F32)).astype(BF16))
+            counted = times * probs
+            d_scores.append((counted * (d_prob - jnp.sum(counted * d_prob, axis=1, keepdims=True))).astype(BF16))
+        for j, q2, d2, weight, d_score in zip(mine, q2s, d2s, weights, d_scores):
+            keep_parted(j * LANES, dot(q2, d_score, (0, 0)).astype(BF16))
+            keep_parted(features + j * LANES, dot(d2, weight, (0, 0)).astype(BF16))
+        swap(batch * planes, planes)
+        swap(nz // 2 + batch * planes, planes)
+        for j, q2, d2, weight, d_score in zip(mine, q2s, d2s, weights, d_scores):
+            span, vspan = spans(j)
+            mixed = dot(weight, kv[:, vspan], (1, 0))
+            attended = jnp.where(low_lane, mixed[:nodes], mixed[nodes:])
+            updated_ref[:, span] = (hidden_ref[:, span].astype(F32) + attended).astype(BF16)
+            partial[:, span] = dot(d_score, q2, (0, 0)).astype(BF16)
+            partial[:, vspan] = dot(weight, d2, (0, 0)).astype(BF16)
 
     outs = [pltpu.make_async_copy(updated_ref, updated_hbm, out_sem.at[0])]
     outs[0].start()
@@ -334,18 +338,6 @@
         first.append((copies_a, copies_b))
         augments.append((augment_a, augment_b, over_a, over_b))
 
-    part = partial[...]
-    for j in range(2):
-        cols = pl.ds(j * half, half)
-        d_norm[:, cols] = dot(part, wkv[cols, :], (1, 1))
-    back_send[0] = d_norm[0:R].astype(BF16)
-    back_send[1] = d_norm[R + rows : window].astype(BF16)
-    back = [
-        remote(back_send.at[0], back_recv.at[0], back_ssem.at[0], back_rsem.at[0], below),
-        remote(back_send.at[1], back_recv.at[1], back_ssem.at[1], back_rsem.at[1], above),
-    ]
-    for copy in back:
-        copy.start()
     def second_exchange(lot, copies_a, copies_b):
         sent_a, sent_b = [], []
         for copy in copies_b:
@@ -405,8 +397,23 @@
         copies_a += augment_a(lot, over_a)
         copies_b += augment_b(lot, over_b)
 
+    part = partial[...]
+    for j in range(2):
+        cols = pl.ds(j * half, half)
+        d_norm[:, cols] = dot(part, wkv[cols, :], (1, 1))
+    back_send[0] = d_norm[0:R].astype(BF16)
+    back_send[1] = d_norm[R + rows : window].astype(BF16)
+    back = [
+        remote(back_send.at[0], back_recv.at[0], back_ssem.at[0], back_rsem.at[0], below),
+        remote(back_send.at[1], back_recv.at[1], back_ssem.at[1], back_rsem.at[1], above),
+    ]
+    for copy in back:
+        copy.start()
     second = [second_exchange(lots[0], *first[0])]
 
+    for lot, copies in zip(lots[1:], first[1:]):
+        second.append(second_exchange(lot, *copies))
+    third = [third_exchange(lot, *copies) for lot, copies in zip(lots, second)]
     for copy in back:
         copy.wait()
     d_norm[R : 2 * R] += back_recv[1].astype(F32)
@@ -421,9 +428,6 @@
     outs.append(pltpu.make_async_copy(dgrid_ref, dgrid_hbm, out_sem.at[1]))
     outs[1].start()
 
-    for lot, copies in zip(lots[1:], first[1:]):
-        second.append(second_exchange(lot, *copies))
-    third = [third_exchange(lot, *copies) for lot, copies in zip(lots, second)]
     for lot, start, copies in zip(lots, starts, third):
         width = lot["kept_a"].shape[-1]
         total = lot["send_z"][z].astype(F32)

time: 46 us -> 43 us (0.935); the launches traced: 45.1 us -> 42.6 us
  Pallas kernels: 44.4 us -> 42 us
    pallas_call x1, Pallas kernels: 42.7 us -> 40.2 us  [per_device(): pl.pallas_call(functools.partial(layer_kernel, sizes, factor), out_shape=...]
where the time goes in v4:
time: 43 us; the launch traced here: 42.6 us
  Pallas kernels  42 us (98%)
  between operations  0.64 us (1%)
    pallas_call x1, Pallas kernels, per_device(): pl.pallas_call(functools.partial(layer_kernel, sizes, factor), out_shape=...  40.2 us
    pallas_call x1, Pallas kernels, per_device(): pl.pallas_call(leave_kernel, out_shape=(jax.ShapeDtypeStruct((nodes, feat...  1.72 us

profile of v4, /device:TPU:1, one launch (start us, length us, event | category | flops | bytes accessed | tf_op | source)
XLA Modules:
  0.0 42.6 jit_solution(14280165814037837425)
XLA Ops:
  0.6 40.2 %encoder_layer.1 = (bf16[32,1024]{1,0:T(8,128)(2,1)}, bf16[128,1024]{1,0:T(8,128)(2,1)}, f32[8,1024]{1,0:T(8,128)}) custom-call(bf16[128,1024]{1,0:T(8,128)(2,1)} %bitcast.9, bf16[32,1024]{1,0:T(8,128)(2,1)} %bitcast.10, bf16[32,1024]{1,0:T(8,128)(2,1)} %bitcast.11, bf16[1024,2048]{1,0:T(8,128)(2,1)} %wkv_hbm.1, bf16[1024,1024]{1,0:T(8,128)(2,1)} %wq_hbm.1, ...), custom_call_target="tpu_custom_call" | custom-call | tf_op jit(solution)/shard_map/encoder_layer/pallas_call | solution.py:547
  40.9 1.7 %leave.1 = (bf16[32,1024]{1,0:T(8,128)(2,1)}, bf16[128,1024]{1,0:T(8,128)(2,1)}, f32[8,1024]{1,0:T(8,128)}) custom-call(bf16[32,1024]{1,0:T(8,128)(2,1)} %get-tuple-element.9.a, bf16[128,1024]{1,0:T(8,128)(2,1)} %get-tuple-element.10.b, f32[8,1024]{1,0:T(8,128)} %get-tuple-element.11.c), custom_call_target="tpu_custom_call" | custom-call | tf_op jit(solution)/shard_map/leave/pallas_call | solution.py:572

commit v5 on v4

--- a/solution.py
+++ b/solution.py
@@ -19,7 +19,7 @@
 F32 = jnp.float32
 BF16 = jnp.bfloat16
 LANES = 128
-WIDTHS = (256, 256)
+WIDTHS = (256, 128, 128)
 
 
 def dot(left, right, contract):
@@ -46,13 +46,9 @@
     q_gain_hbm,
     index_hbm,
     mask_hbm,
-    updated_hbm,
-    dgrid_hbm,
-    dw_hbm,
     updated_ref,
     dgrid_ref,
     dw_ref,
-    out_sem,
     grid_ref,
     hidden_ref,
     cot_ref,
@@ -61,6 +57,8 @@
     index_ref,
     mask_ref,
     edge,
+    pairs,
+    inner,
     wkv,
     wq,
     standard,
@@ -91,7 +89,7 @@
     nodes, features = hidden_hbm.shape
     window = rows + 2 * R
     half = features // 2
-    own = dw_hbm.shape[0]
+    own = dw_ref.shape[0]
 
     z, x = lax.axis_index("bz"), lax.axis_index("bx")
     c, y = lax.axis_index("bc"), lax.axis_index("ens")
@@ -156,7 +154,7 @@
     hat, scale = normalize(grid_ref[...].astype(F32))
     standard[...] = hat
     inv_std[...] = scale
-    win[R : R + rows] = (hat * src_gain_ref[...]).astype(BF16)
+    win[:rows] = (hat * src_gain_ref[...]).astype(BF16)
 
     load_hidden.wait()
     load_q_gain.wait()
@@ -171,6 +169,7 @@
     local = index_ref[...] - (band * rows - R)
     local = jnp.where(mask_ref[...] > 0, local, -1)
     row_ids = lax.broadcasted_iota(jnp.int32, (window, nodes), 0)
+    row_ids = jnp.where(row_ids < rows, row_ids + R, jnp.where(row_ids < rows + R, row_ids - rows, row_ids))
     times = jnp.zeros((window, nodes), F32)
     for j in range(K):
         times = times + jnp.where(local[j : j + 1, :] == row_ids, 1.0, 0.0)
@@ -180,21 +179,8 @@
 
     for j, cols in enumerate(quarter):
         load_kv[j].wait()
-        kv[R : R + rows, cols] = dot(win[R : R + rows], wkv[:, cols], (1, 0)).astype(BF16)
-    for copy in halo:
-        copy.wait_recv()
-    hat, _ = normalize(edge[...].reshape(2 * R, features).astype(F32))
-    outer = (hat * src_gain_ref[...]).astype(BF16)
-    win[0:R] = outer[:R]
-    win[R + rows : window] = outer[R:]
-    swap_win = remote(win, pair_win, win_send, win_recv, pair)
-    swap_win.start()
-    for cols in quarter:
-        tile = dot(outer, wkv[:, cols], (1, 0)).astype(BF16)
-        kv[0:R, cols] = tile[:R]
-        kv[R + rows : window, cols] = tile[R:]
+        kv[:rows, cols] = dot(win[:rows], wkv[:, cols], (1, 0)).astype(BF16)
     load_cot.wait()
-
     low_lane = lax.broadcasted_iota(jnp.int32, (nodes, LANES), 1) < features // HEADS
     cot = cot_ref[...]
     zero = jnp.zeros((nodes, LANES), F32)
@@ -205,6 +191,26 @@
             [jnp.where(low_lane, block, zero), jnp.where(low_lane, zero, block)], axis=0
         ).astype(BF16)
 
+    def spans(j):
+        return slice(j * LANES, (j + 1) * LANES), slice(features + j * LANES, features + (j + 1) * LANES)
+
+    for j in range(features // LANES):
+        span, vspan = spans(j)
+        q2 = two_heads(queries[:, span])
+        d2 = two_heads(cot[:, span])
+        pairs[0, j], pairs[1, j] = q2, d2
+        inner[0, j] = dot(q2, kv[:rows, span], (1, 1))
+        inner[1, j] = dot(d2, kv[:rows, vspan], (1, 1))
+
+    for copy in halo:
+        copy.wait_recv()
+    hat, _ = normalize(edge[...].reshape(2 * R, features).astype(F32))
+    outer = (hat * src_gain_ref[...]).astype(BF16)
+    win[rows:] = outer
+    swap_win = remote(win, pair_win, win_send, win_recv, pair)
+    swap_win.start()
+    for cols in quarter:
+        kv[rows:, cols] = dot(outer, wkv[:, cols], (1, 0)).astype(BF16)
     group = ny * own
 
     swaps = []
@@ -231,15 +237,16 @@
     batches = 2 if nz >= 4 else 1
     blocks = features // LANES
     planes = nz // (2 * batches)
-    def spans(j):
-        return slice(j * LANES, (j + 1) * LANES), slice(features + j * LANES, features + (j + 1) * LANES)
-
     for batch in range(batches):
         mine = range(batch * blocks // batches, (batch + 1) * blocks // batches)
-        q2s = [two_heads(queries[:, spans(j)[0]]) for j in mine]
-        d2s = [two_heads(cot[:, spans(j)[0]]) for j in mine]
-        scores = [dot(q2, kv[:, spans(j)[0]], (1, 1)) for q2, j in zip(q2s, mine)]
-        d_probs = [dot(d2, kv[:, spans(j)[1]], (1, 1)) for d2, j in zip(d2s, mine)]
+        q2s = [pairs[0, j] for j in mine]
+        d2s = [pairs[1, j] for j in mine]
+        scores = [
+            jnp.concatenate([inner[0, j], dot(q2, kv[rows:, spans(j)[0]], (1, 1))], axis=1) for q2, j in zip(q2s, mine)
+        ]
+        d_probs = [
+            jnp.concatenate([inner[1, j], dot(d2, kv[rows:, spans(j)[1]], (1, 1))], axis=1) for d2, j in zip(d2s, mine)
+        ]
         weights, d_scores = [], []
         for score, d_prob in zip(scores, d_probs):
             shifted = jnp.where(live, score, -jnp.inf)
@@ -261,8 +268,6 @@
             partial[:, span] = dot(d_score, q2, (0, 0)).astype(BF16)
             partial[:, vspan] = dot(weight, d2, (0, 0)).astype(BF16)
 
-    outs = [pltpu.make_async_copy(updated_ref, updated_hbm, out_sem.at[0])]
-    outs[0].start()
     swap_win.wait()
     for copy in swaps:
         copy.wait()
@@ -387,7 +392,7 @@
         for j in range(ny - 1):
             total = total + lot["recv_a2"][j].astype(F32)
         send[:, :, :width] = total.astype(BF16)
-        for k in range(1, nz):
+        for k in sorted(range(1, nz), key=lambda k: abs(2 * k - nz)):
             i, src = k - 1, send.at[(z + k) % nz]
             sent.append(remote(src, lot["recv_z"].at[i], lot["z_ssem"].at[i], lot["z_rsem"].at[i], z_peer(k)))
             sent[-1].start()
@@ -401,8 +406,8 @@
     for j in range(2):
         cols = pl.ds(j * half, half)
         d_norm[:, cols] = dot(part, wkv[cols, :], (1, 1))
-    back_send[0] = d_norm[0:R].astype(BF16)
-    back_send[1] = d_norm[R + rows : window].astype(BF16)
+    back_send[0] = d_norm[rows : rows + R].astype(BF16)
+    back_send[1] = d_norm[rows + R : window].astype(BF16)
     back = [
         remote(back_send.at[0], back_recv.at[0], back_ssem.at[0], back_rsem.at[0], below),
         remote(back_send.at[1], back_recv.at[1], back_ssem.at[1], back_rsem.at[1], above),
@@ -416,49 +421,38 @@
     third = [third_exchange(lot, *copies) for lot, copies in zip(lots, second)]
     for copy in back:
         copy.wait()
-    d_norm[R : 2 * R] += back_recv[1].astype(F32)
-    d_norm[rows : rows + R] += back_recv[0].astype(F32)
-    dx = d_norm[R : R + rows] * src_gain_ref[...]
+    d_norm[:R] += back_recv[1].astype(F32)
+    d_norm[rows - R : rows] += back_recv[0].astype(F32)
+    dx = d_norm[:rows] * src_gain_ref[...]
     hat = standard[...]
     dgrid_ref[...] = (
         inv_std[...]
         * (dx - jnp.mean(dx, axis=-1, keepdims=True) - hat * jnp.mean(dx * hat, axis=-1, keepdims=True))
     ).astype(BF16)
 
-    outs.append(pltpu.make_async_copy(dgrid_ref, dgrid_hbm, out_sem.at[1]))
-    outs[1].start()
 
     for lot, start, copies in zip(lots, starts, third):
         width = lot["kept_a"].shape[-1]
         total = lot["send_z"][z].astype(F32)
+        for copy in copies:
+            copy.wait()
         for k in range(1, nz):
-            copies[k - 1].wait()
             total = total + lot["recv_z"][k - 1].astype(F32)
         total = total * factor
         dw_ref[:, start : start + width] = total[:, :width]
         dw_ref[:, half + start : half + start + width] = total[:, width:]
-    outs.append(pltpu.make_async_copy(dw_ref, dw_hbm, out_sem.at[2]))
-    outs[2].start()
-    for copy in outs:
-        copy.wait()
     for copy in halo:
         copy.wait_send()
 
 
-def leave_kernel(a, b, c, a_out, b_out, c_out, a_held, b_held, c_held, sem):
-    into = [
-        pltpu.make_async_copy(src, dst, sem.at[i]) for i, (src, dst) in enumerate([(b, b_held), (a, a_held), (c, c_held)])
+def leave_kernel(a, b, c, a_out, b_out, c_out, sem):
+    copies = [
+        pltpu.make_async_copy(src, dst, sem.at[i])
+        for i, (src, dst) in enumerate([(b, b_out), (a, a_out), (c, c_out)])
     ]
-    out = [
-        pltpu.make_async_copy(src, dst, sem.at[3 + i])
-        for i, (src, dst) in enumerate([(b_held, b_out), (a_held, a_out), (c_held, c_out)])
-    ]
-    for copy in into:
+    for copy in copies:
         copy.start()
-    for first, second in zip(into, out):
-        first.wait()
-        second.start()
-    for copy in out:
+    for copy in copies:
         copy.wait()
 
 
@@ -508,10 +502,6 @@
             )
         )
     scratch = [
-        V((nodes, features), BF16),
-        V((rows, features), BF16),
-        V((own, features), F32),
-        dma((3,)),
         V((rows, features), BF16),
         V((nodes, features), BF16),
         V((nodes, features), BF16),
@@ -520,6 +510,8 @@
         V((K, nodes), jnp.int32),
         V((K, nodes), jnp.int32),
         V((2, R, features), BF16),
+        V((2, features // LANES, 2 * nodes, LANES), BF16),
+        V((2, features // LANES, 2 * nodes, rows), F32),
         V((features, columns), BF16),
         V((features, features), BF16),
         V((rows, features), F32),
@@ -544,21 +536,7 @@
         dma((2,)),
         dma((2,)),
     ]
-    updated, d_grid, d_wkv_t = pl.pallas_call(
-        functools.partial(layer_kernel, sizes, factor),
-        out_shape=(
-            jax.ShapeDtypeStruct((nodes, features), BF16),
-            jax.ShapeDtypeStruct((rows, features), BF16),
-            jax.ShapeDtypeStruct((own, features), F32),
-        ),
-        in_specs=[hbm] * 9,
-        out_specs=(hbm, hbm, hbm),
-        scratch_shapes=scratch,
-        compiler_params=pltpu.CompilerParams(
-            collective_id=0, has_side_effects=True, vmem_limit_bytes=60 * 1024 * 1024
-        ),
-        name="encoder_layer",
-    )(
+    inputs = (
         grid_latent[0],
         hidden[0],
         d_updated[0],
@@ -570,21 +548,33 @@
         edge_mask.T,
     )
     updated, d_grid, d_wkv_t = pl.pallas_call(
+        functools.partial(layer_kernel, sizes, factor),
+        out_shape=(
+            jax.ShapeDtypeStruct((nodes, features), BF16),
+            jax.ShapeDtypeStruct((rows, features), BF16),
+            jax.ShapeDtypeStruct((own, features), F32),
+        ),
+        in_specs=[hbm] * 9,
+        out_specs=(vmem, vmem, vmem),
+        scratch_shapes=scratch,
+        compiler_params=pltpu.CompilerParams(
+            collective_id=0, has_side_effects=True, vmem_limit_bytes=52 * 1024 * 1024
+        ),
+        name="encoder_layer",
+    )(
+        *[pltpu.with_memory_space_constraint(value, pltpu.HBM) for value in inputs]
+    )
+    updated, d_grid, d_wkv_t = pl.pallas_call(
         leave_kernel,
         out_shape=(
             jax.ShapeDtypeStruct((nodes, features), BF16),
             jax.ShapeDtypeStruct((rows, features), BF16),
             jax.ShapeDtypeStruct((own, features), F32),
         ),
-        in_specs=[hbm, hbm, hbm],
+        in_specs=[vmem, vmem, vmem],
         out_specs=(hbm, hbm, hbm),
-        scratch_shapes=[
-            V((nodes, features), BF16),
-            V((rows, features), BF16),
-            V((own, features), F32),
-            dma((6,)),
-        ],
-        compiler_params=pltpu.CompilerParams(vmem_limit_bytes=60 * 1024 * 1024),
+        scratch_shapes=[dma((3,))],
+        compiler_params=pltpu.CompilerParams(vmem_limit_bytes=2 * 1024 * 1024),
         name="leave",
     )(updated, d_grid, d_wkv_t)
     return (updated[None], d_grid[None], d_wkv_t)

time: 43 us -> 40.6 us (0.944)
  Pallas kernels: 42 us -> 39.9 us
    pallas_call x1, Pallas kernels: 40.2 us -> 39.1 us  [per_device(): pl.pallas_call(functools.partial(layer_kernel, sizes, factor), out_shape=...]
    pallas_call x1, Pallas kernels: 1.72 us -> 0.75 us  [per_device(): pl.pallas_call(leave_kernel, out_shape=(jax.ShapeDtypeStruct((nodes, feat...]
where the time goes in v5:
time: 40.6 us; the launch traced here: 40.5 us
  Pallas kernels  39.9 us (98%)
  between operations  0.64 us (2%)
    pallas_call x1, Pallas kernels, per_device(): pl.pallas_call(functools.partial(layer_kernel, sizes, factor), out_shape=...  39.1 us

profile of v5, /device:TPU:1, one launch (start us, length us, event | category | flops | bytes accessed | tf_op | source)
XLA Modules:
  0.0 40.5 jit_solution(18093170398636985235)
XLA Ops:
  0.6 39.1 %encoder_layer.1 = (bf16[32,1024]{1,0:T(8,128)(2,1)S(1)}, bf16[128,1024]{1,0:T(8,128)(2,1)S(1)}, f32[8,1024]{1,0:T(8,128)S(1)}) custom-call(bf16[128,1024]{1,0:T(8,128)(2,1)} %bitcast.9, bf16[32,1024]{1,0:T(8,128)(2,1)} %bitcast.10, bf16[32,1024]{1,0:T(8,128)(2,1)} %bitcast.11, bf16[1024,2048]{1,0:T(8,128)(2,1)} %wkv_hbm.1, bf16[1024,1024]{1,0:T(8,128)(2,1)} %wq_hbm.1, ...), custom_call_target="tpu_custom_call" | custom-call | tf_op jit(solution)/shard_map/encoder_layer/pallas_call | solution.py:550
  39.8 0.8 %leave.1 = (bf16[32,1024]{1,0:T(8,128)(2,1)}, bf16[128,1024]{1,0:T(8,128)(2,1)}, f32[8,1024]{1,0:T(8,128)}) custom-call(bf16[32,1024]{1,0:T(8,128)(2,1)S(1)} %get-tuple-element.9.a, bf16[128,1024]{1,0:T(8,128)(2,1)S(1)} %get-tuple-element.10.b, f32[8,1024]{1,0:T(8,128)S(1)} %get-tuple-element.11.c), custom_call_target="tpu_custom_call" | custom-call | tf_op jit(solution)/shard_map/leave/pallas_call | solution.py:567

commit v6 on v5

--- a/solution.py
+++ b/solution.py
@@ -19,7 +19,7 @@
 F32 = jnp.float32
 BF16 = jnp.bfloat16
 LANES = 128
-WIDTHS = (256, 128, 128)
+WIDTHS = (256, 256)
 
 
 def dot(left, right, contract):
@@ -402,6 +402,10 @@
         copies_a += augment_a(lot, over_a)
         copies_b += augment_b(lot, over_b)
 
+    second = [second_exchange(lots[0], *first[0])]
+
+    for lot, copies in zip(lots[1:], first[1:]):
+        second.append(second_exchange(lot, *copies))
     part = partial[...]
     for j in range(2):
         cols = pl.ds(j * half, half)
@@ -414,10 +418,6 @@
     ]
     for copy in back:
         copy.start()
-    second = [second_exchange(lots[0], *first[0])]
-
-    for lot, copies in zip(lots[1:], first[1:]):
-        second.append(second_exchange(lot, *copies))
     third = [third_exchange(lot, *copies) for lot, copies in zip(lots, second)]
     for copy in back:
         copy.wait()

time: 40.6 us -> 40.6 us (level)
  no operation moved by 1% of the time
where the time goes in v6:
time: 40.6 us
  Pallas kernels  39.9 us (98%)
  between operations  0.64 us (2%)
    pallas_call x1, Pallas kernels, per_device(): pl.pallas_call(functools.partial(layer_kernel, sizes, factor), out_shape=...  39.2 us

profile of v6, /device:TPU:1, one launch (start us, length us, event | category | flops | bytes accessed | tf_op | source)
XLA Modules:
  0.0 40.6 jit_solution(10868663361953128954)
XLA Ops:
  0.6 39.2 %encoder_layer.1 = (bf16[32,1024]{1,0:T(8,128)(2,1)S(1)}, bf16[128,1024]{1,0:T(8,128)(2,1)S(1)}, f32[8,1024]{1,0:T(8,128)S(1)}) custom-call(bf16[128,1024]{1,0:T(8,128)(2,1)} %bitcast.9, bf16[32,1024]{1,0:T(8,128)(2,1)} %bitcast.10, bf16[32,1024]{1,0:T(8,128)(2,1)} %bitcast.11, bf16[1024,2048]{1,0:T(8,128)(2,1)} %wkv_hbm.1, bf16[1024,1024]{1,0:T(8,128)(2,1)} %wq_hbm.1, ...), custom_call_target="tpu_custom_call" | custom-call | tf_op jit(solution)/shard_map/encoder_layer/pallas_call | solution.py:550
  39.8 0.8 %leave.1 = (bf16[32,1024]{1,0:T(8,128)(2,1)}, bf16[128,1024]{1,0:T(8,128)(2,1)}, f32[8,1024]{1,0:T(8,128)}) custom-call(bf16[32,1024]{1,0:T(8,128)(2,1)S(1)} %get-tuple-element.9.a, bf16[128,1024]{1,0:T(8,128)(2,1)S(1)} %get-tuple-element.10.b, f32[8,1024]{1,0:T(8,128)S(1)} %get-tuple-element.11.c), custom_call_target="tpu_custom_call" | custom-call | tf_op jit(solution)/shard_map/leave/pallas_call | solution.py:567
